TPU v7x, 128 devices: a whole 4x4x4 slice. The times are simulated.
128 devices in a mesh: ax: 8 (over y, z_lo), az: 16 (over z_hi, x, core).
Axes of the slice: x: 4, y: 4, z: 4 (z_hi: 2, z_lo: 2; z = z_hi * 2 + z_lo), core: 2. Of those that a mesh axis runs over, the one named last changes fastest.
Arguments:
- saved_flow: float32 [3, 256, 64, 1024], P(None, 'az', None, 'ax'), may hold values from -6 to 6
- saved_adjoint: float32 [3, 256, 64, 1024], P(None, 'az', None, 'ax'), may hold values from -6 to 6
- tangent: float32 [3, 256, 64, 1024], P(None, 'az', None, 'ax'), may hold values from -6 to 6
- second_adjoint: float32 [3, 256, 64, 1024], P(None, 'az', None, 'ax'), may hold values from -6 to 6
- radial_rate: float32 [64], replicated, may hold values from 1 to 100
Outputs:
- tangent_next: float32 [3, 256, 64, 1024], P(None, 'az', None, 'ax')
- second_next: float32 [3, 256, 64, 1024], P(None, 'az', None, 'ax')
All inputs are finite; a program needn't handle non-finite values.
Results may differ from a plain program's by a relative error of at most 0.00005.
Values sent between devices are 32-bit elements; how exact they have to be, the bound alone decides.
No kernel may reach another device: no remote copies, remote signals or barrier semaphores. Data moves between devices by JAX's collectives and lax.ppermute only.
A program may use at most 128 MiB of HBM per device.

v0:
```python
import math

import jax
import jax.numpy as jnp
from jax import lax
from jax.sharding import PartitionSpec as P

time_step = 0.1
viscosity = 0.005
axial_unit = 2.0 * math.pi / 20.0


def radial_table(count):
    points = jnp.arange(count, dtype=jnp.int32)[:, None]
    orders = jnp.arange(count, dtype=jnp.int32)[None, :]
    phases = orders * (2 * points + 1) % (4 * count)
    values = jnp.cos(phases.astype(jnp.float32) * (math.pi / (2.0 * count)))
    scales = jnp.where(orders == 0, math.sqrt(1.0 / count), math.sqrt(2.0 / count))
    return values * scales


def hartley_table(length):
    row_index = jnp.arange(length, dtype=jnp.int32)[:, None]
    col_index = jnp.arange(length, dtype=jnp.int32)[None, :]
    phases = row_index * col_index % length
    angles = phases.astype(jnp.float32) * (2.0 * math.pi / length)
    return (jnp.cos(angles) + jnp.sin(angles)) / math.sqrt(length)


def body(saved_flow, saved_adjoint, tangent, second_adjoint, radial_rate):
    components = tangent.shape[0]
    local_azimuth = tangent.shape[1]
    radial_count = tangent.shape[2]
    local_axial = tangent.shape[3]
    azimuth_count = local_azimuth * lax.axis_size("az")
    axial_count = local_axial * lax.axis_size("ax")
    radial = radial_table(radial_count)
    azimuth_table = hartley_table(azimuth_count)
    axial_table = hartley_table(axial_count)

    def along_azimuth(field):
        return jnp.einsum("nm,cmjk->cnjk", azimuth_table, field, precision=lax.Precision.HIGHEST)

    def along_axial(field):
        return jnp.einsum("nk,cmjk->cmjn", axial_table, field, precision=lax.Precision.HIGHEST)

    stacked = jnp.concatenate((saved_flow, saved_adjoint, tangent, second_adjoint), axis=0)
    grid = jnp.einsum("jr,cmrk->cmjk", radial, stacked, precision=lax.Precision.HIGHEST)
    halfway = along_azimuth(lax.all_to_all(grid, "az", split_axis=2, concat_axis=1, tiled=True))
    physical = along_axial(lax.all_to_all(halfway, "ax", split_axis=1, concat_axis=3, tiled=True))
    flow = physical[0:components]
    adjoint = physical[components : 2 * components]
    tang = physical[2 * components : 3 * components]
    second = physical[3 * components : 4 * components]
    flow_sum = jnp.sum(flow, axis=0)[None]
    adjoint_sum = jnp.sum(adjoint, axis=0)[None]
    tang_sum = jnp.sum(tang, axis=0)[None]
    second_sum = jnp.sum(second, axis=0)[None]
    tangent_rhs = flow * tang_sum + tang * flow_sum
    second_rhs = flow * second_sum + second * flow_sum + adjoint * tang_sum + tang * adjoint_sum
    products = jnp.concatenate((tangent_rhs, second_rhs), axis=0)
    partial_field = along_axial(products)
    turned = along_azimuth(
        lax.all_to_all(partial_field, "ax", split_axis=3, concat_axis=1, tiled=True)
    )
    spectral = jnp.einsum(
        "jr,cmjk->cmrk",
        radial,
        lax.all_to_all(turned, "az", split_axis=1, concat_axis=2, tiled=True),
        precision=lax.Precision.HIGHEST,
    )
    azimuth = lax.axis_index("az") * local_azimuth + jnp.arange(local_azimuth, dtype=jnp.int32)
    wave_azimuth = jnp.minimum(azimuth, azimuth_count - azimuth).astype(jnp.float32)
    axial = lax.axis_index("ax") * local_axial + jnp.arange(local_axial, dtype=jnp.int32)
    wave_axial = jnp.minimum(axial, axial_count - axial).astype(jnp.float32) * axial_unit
    total = (
        radial_rate[None, :, None]
        + (wave_azimuth**2)[:, None, None]
        + (wave_axial**2)[None, None, :]
    )
    denom = (1.0 + viscosity * total)[None]
    tangent_next = (tangent + time_step * spectral[0:components]) / denom
    second_next = (second_adjoint + time_step * spectral[components : 2 * components]) / denom
    return (tangent_next, second_next)


def solution(mesh):
    in_specs = (
        P(None, "az", None, "ax"),
        P(None, "az", None, "ax"),
        P(None, "az", None, "ax"),
        P(None, "az", None, "ax"),
        P(),
    )
    out_specs = (P(None, "az", None, "ax"), P(None, "az", None, "ax"))
    return jax.shard_map(body, mesh=mesh, in_specs=in_specs, out_specs=out_specs, check_vma=False)
```

profile of v0, /device:TPU:1, one launch (start us, length us, event | category | flops | bytes accessed | tf_op | source)
XLA Modules:
  0.0 556.8 jit_solution(827337466593299157)
XLA Ops:
  0.7 8.1 %fusion.23 = f32[12,16,64,128]{3,2,1,0:T(8,128)S(1)} fusion(f32[3,16,64,128]{3,2,1,0:T(8,128)} %param.8, f32[3,16,64,128]{3,2,1,0:T(8,128)} %param.7, f32[3,16,64,128]{3,2,1,0:T(8,128)} %param.6, f32[3,16,64,128]{3,2,1,0:T(8,128)} %param.5, f32[64]{0:T(128)S(1)} %compare_select_fusion, s32[64]{0:T(128)S(1)} %multiply_add_fusion.3), kind=kOutput, calls=%fused_computation.27 | convolution fusion | flops 1212739584 | bytes 12583424 | tf_op jit(solution)/shard_map/jr,cmrk->cmjk/dot_general | solution.py:48
  8.8 3.6 copy.33
  12.4 82.0 %all_to_all.72 = f32[12,16,64,128]{3,1,0,2:T(8,128)S(1)} all-to-all(f32[12,16,64,128]{3,1,0,2:T(8,128)S(1)} %copy.33), channel_id=1, replica_groups=mesh['ax'=8,'az'=16] {'az'}, dimensions={2} | all-to-all | bytes 12582912 | tf_op jit(solution)/shard_map/all_to_all | solution.py:49
  95.3 14.3 %convolution_bitcast_fusion = f32[12,256,4,128]{1,3,2,0:T(8,128)} fusion(f32[12,256,4,128]{3,1,2,0:T(8,128)S(1)} %bitcast.66), kind=kOutput, calls=%fused_computation.28 | convolution fusion | flops 4832886784 | bytes 12582912 | tf_op jit(solution)/shard_map/nm,cmjk->cnjk/dot_general | solution.py:42
  109.6 7.9 %copy.37 = f32[12,256,4,128]{3,2,0,1:T(4,128)} copy(f32[12,256,4,128]{1,3,2,0:T(8,128)} %convolution_bitcast_fusion) | data formatting | bytes 12582912 | tf_op jit(solution)/shard_map/nm,cmjk->cnjk/transpose | solution.py:42
  117.5 5.0 all-to-all-start.1
  122.5 17.7 %fusion.108 = f32[1024,1024,1,1]{1,0,3,2:T(8,128)} fusion(), kind=kLoop, calls=%fused_computation.19.clone.1 | loop fusion | flops 16777216 | bytes 4194304 | tf_op jit(solution)/shard_map/nk,cmjk->cmjn/dot_general | solution.py:45
  140.2 69.0 %all-to-all-done.1 = f32[12,256,4,128]{3,2,0,1:T(4,128)} async-done(((f32[12,256,4,128]{3,2,0,1:T(4,128)}), f32[12,256,4,128]{3,2,0,1:T(4,128)}, u32[]{:S(2)}, u32[]{:S(2)}) %all-to-all-start.1) | async-done | bytes 6291488 | tf_op jit(solution)/shard_map/all_to_all | solution.py:50
  209.2 5.0 copy.38
  214.2 144.5 %fusion = f32[12,32,4,1024]{3,1,2,0:T(8,128)S(1)} fusion(f32[12,4,8,4,8,128]{5,4,3,2,1,0:T(8,128)S(1)} %bitcast.70, f32[1024,1024,1,1]{1,0,3,2:T(8,128)S(1)} %copy-done.2), kind=kOutput, calls=%fused_computation | convolution fusion | flops 19327352832 | bytes 16777216 | tf_op jit(solution)/shard_map/nk,cmjk->cmjn/dot_general | solution.py:45
  361.1 29.0 %fusion.14 = f32[6,32,4,1024]{3,1,2,0:T(8,128)S(1)} fusion(f32[6,32,4,1024]{3,1,2,0:T(8,128)S(1)} %fusion.110), kind=kOutput, calls=%fused_computation.17 | convolution fusion | flops 9680453632 | bytes 6291456 | tf_op jit(solution)/shard_map/nk,cmjk->cmjn/dot_general | solution.py:45
  390.1 9.1 %copy.40 = f32[6,32,4,1024]{1,2,0,3:T(4,128)} copy(f32[6,32,4,1024]{3,1,2,0:T(8,128)S(1)} %fusion.14) | data formatting | bytes 6291456 | tf_op jit(solution)/shard_map/nk,cmjk->cmjn/dot_general | solution.py:45
  399.2 12.3 %reshape.77 = f32[8,1,98304]{2,1,0:T(1,128)} reshape(f32[1024,6,4,32]{3,2,1,0:T(4,128)} %bitcast.63) | data formatting | bytes 6291456
  411.5 39.0 %all_to_all.73 = f32[8,1,98304]{2,1,0:T(1,128)S(1)} all-to-all(f32[8,1,98304]{2,1,0:T(1,128)} %reshape.77), channel_id=1, replica_groups=mesh['ax'=8,'az'=16] {'ax'}, dimensions={0} | all-to-all | bytes 6291456 | tf_op jit(solution)/shard_map/all_to_all | solution.py:64
  451.0 11.1 %reduce = f32[8,98304]{1,0:T(8,128)} reduce(f32[8,1,98304]{2,1,0:T(1,128)S(1)} %all_to_all.73, f32[]{:T(128)} %broadcast.149), dimensions={1}, to_apply=%all_to_all.60.reduce_sub_computation | reduce | bytes 6291460 | tf_op jit(solution)/shard_map/all_to_all | solution.py:64
  462.1 13.3 %reshape.78 = f32[1024,6,4,32]{3,2,1,0:T(4,128)} reshape(f32[8,98304]{1,0:T(8,128)} %reduce) | data formatting | bytes 6291456
  475.4 11.4 %copy.56 = f32[6,32,4,8,128]{4,1,3,2,0:T(8,128)} copy(f32[6,32,4,8,128]{1,2,0,4,3:T(4,128)} %bitcast.64) | data formatting | bytes 6291456 | tf_op jit(solution)/shard_map/all_to_all | solution.py:64
  486.8 7.9 %convolution_bitcast_fusion.2 = f32[6,256,4,128]{1,3,2,0:T(8,128)S(1)} fusion(f32[6,256,4,128]{3,1,2,0:T(8,128)} %bitcast.69), kind=kOutput, calls=%fused_computation.30 | convolution fusion | flops 2416967680 | bytes 6291456 | tf_op jit(solution)/shard_map/nm,cmjk->cnjk/dot_general | solution.py:42
  494.7 3.0 copy.44
  497.7 8.5 %all-to-all-start.3 = ((f32[6,256,4,128]{3,2,0,1:T(4,128)}), f32[6,256,4,128]{3,2,0,1:T(4,128)S(1)}, u32[]{:S(2)}, u32[]{:S(2)}) async-start(f32[6,256,4,128]{3,2,0,1:T(4,128)} %copy.44), calls=%async_computation.3 | async-start | bytes 6291456 | tf_op jit(solution)/shard_map/all_to_all | solution.py:69
  507.3 40.6 %all-to-all-done.3 = f32[6,256,4,128]{3,2,0,1:T(4,128)S(1)} async-done(((f32[6,256,4,128]{3,2,0,1:T(4,128)}), f32[6,256,4,128]{3,2,0,1:T(4,128)S(1)}, u32[]{:S(2)}, u32[]{:S(2)}) %all-to-all-start.3) | async-done | bytes 3145760 | tf_op jit(solution)/shard_map/all_to_all | solution.py:69
  548.5 2.0 copy.46
  550.6 3.3 convolution_bitcast_fusion.1
  553.9 2.5 fusion.27
  (22 shorter events, 5.5 us)
Async XLA Ops:
  117.5 91.7 %all-to-all-start.1 = ((f32[12,256,4,128]{3,2,0,1:T(4,128)}), f32[12,256,4,128]{3,2,0,1:T(4,128)}, u32[]{:S(2)}, u32[]{:S(2)}) async-start(f32[12,256,4,128]{3,2,0,1:T(4,128)} %copy.37), calls=%async_computation.1 | async-start | bytes 12582912 | tf_op jit(solution)/shard_map/all_to_all | solution.py:50
  209.2 5.0 copy-start.2
  497.7 8.5 %copy-start.4 = (f32[64]{0:T(128)S(1)}, f32[64]{0:T(128)}, u32[]{:S(2)}) copy-start(f32[64]{0:T(128)} %param.9) | copy-start | bytes 772
  497.7 50.2 %all-to-all-start.3 = ((f32[6,256,4,128]{3,2,0,1:T(4,128)}), f32[6,256,4,128]{3,2,0,1:T(4,128)S(1)}, u32[]{:S(2)}, u32[]{:S(2)}) async-start(f32[6,256,4,128]{3,2,0,1:T(4,128)} %copy.44), calls=%async_computation.3 | async-start | bytes 6291456 | tf_op jit(solution)/shard_map/all_to_all | solution.py:69
  550.6 3.3 copy-start
  550.6 3.3 copy-start.1
  550.6 3.3 copy-start.3
where the time goes:
time: 563 us; the launch traced here: 557 us
  matrix products  207 us (37%)
  blocking collectives  121 us (21%)
  waiting for transfers between devices  110 us (20%)
  local copies, waits for them, and re-layouts  69.6 us (12%)
  other arithmetic  34.8 us (6%)
  starting transfers between devices  13.5 us (2%)
    dot_general x2, matrix products, along_axial(): jnp.einsum('nk,cmjk->cmjn', axial_table, field, precision=lax.Precision.H...  174 us
    all_to_all x1, blocking collectives, body(): lax.all_to_all(grid, 'az', split_axis=2, concat_axis=1, tiled=True)  82 us
    all_to_all x1, waiting for transfers between devices, body(): lax.all_to_all(halfway, 'ax', split_axis=1, concat_axis=3, tiled=True)  69 us
    all_to_all x1, waiting for transfers between devices, body(): lax.all_to_all(turned, 'az', split_axis=1, concat_axis=2, tiled=True)  40.6 us
    all_to_all x1, blocking collectives, body(): lax.all_to_all(partial_field, 'ax', split_axis=3, concat_axis=1, tiled=True)  39 us
    unnamed x12, local copies, waits for them, and re-layouts  25.6 us
    dot_general x2, matrix products, along_azimuth(): jnp.einsum('nm,cmjk->cnjk', azimuth_table, field, precision=lax.Precision...  22.2 us
    dot_general x2, other arithmetic, along_axial(): jnp.einsum('nk,cmjk->cmjn', axial_table, field, precision=lax.Precision.H...  17.9 us
  transfers between devices with their start and end apart: 2, of which 2 were waited for; matrix products, arithmetic and copies ran while one was open for 3% of the time, Pallas kernels for 0%

commit v1 on v0

v1 whole, which is shorter than its diff:
```python
import math

import jax
import jax.numpy as jnp
import numpy as np
from jax import lax
from jax.experimental import pallas as pl
from jax.experimental.pallas import tpu as pltpu
from jax.sharding import PartitionSpec as P

time_step = 0.1
viscosity = 0.005
axial_unit = 2.0 * math.pi / 20.0
F32 = jnp.float32
BF16 = jnp.bfloat16


def radial_table(count):
    points = np.arange(count)[:, None]
    orders = np.arange(count)[None, :]
    phases = orders * (2 * points + 1) % (4 * count)
    scales = np.where(orders == 0, math.sqrt(1.0 / count), math.sqrt(2.0 / count))
    return np.cos(phases * (math.pi / (2.0 * count))) * scales


def hartley_table(rows, cols, length):
    angles = (rows[:, None] * cols[None, :] % length) * (2.0 * math.pi / length)
    return (np.cos(angles) + np.sin(angles)) / math.sqrt(length)


def halves(table):
    table = np.asarray(table, np.float32)
    high = table.astype(BF16)
    low = (table - high.astype(np.float32)).astype(BF16)
    return np.stack((high, low))


def split(x):
    high = x.astype(BF16)
    return high, (x - high.astype(F32)).astype(BF16)


def table_dot(table, x):
    high, low = split(x)
    left = jnp.concatenate((table[0], table[0], table[1]), axis=1)
    right = jnp.concatenate((high, low, high), axis=0)
    return jnp.dot(left, right, preferred_element_type=F32)


def dot_table(x, table, turned):
    high, low = split(x)
    left = jnp.concatenate((high, low, high), axis=1)
    right = jnp.concatenate((table[0], table[0], table[1]), axis=1 if turned else 0)
    return lax.dot_general(
        left, right, (((1,), (1 if turned else 0,)), ((), ())), preferred_element_type=F32
    )


def spread_kernel(first_ref, second_ref, wide_ref, out_ref, table_ref):
    radial = wide_ref.shape[0]
    rows = radial * 8
    lane = lax.broadcasted_iota(jnp.int32, (8, rows), 1) // radial
    keep = lane == lax.broadcasted_iota(jnp.int32, (8, rows), 0)
    for j in range(radial):
        block = jnp.where(keep, jnp.broadcast_to(wide_ref[j : j + 1, :], (8, rows)), 0.0)
        high, low = split(block)
        table_ref[0, 8 * j : 8 * j + 8, :] = high
        table_ref[1, 8 * j : 8 * j + 8, :] = low
    table = (table_ref[0], table_ref[1])

    def step(index, _):
        c, group = index // 2, index % 2
        start = pl.multiple_of(group * 8, 8)
        x = jnp.concatenate(
            [ref[c, pl.ds(start, 8)].reshape(rows, 128) for ref in (first_ref, second_ref)], axis=1
        )
        y = table_dot(table, x)
        for core in range(2):
            out_ref[:, core, c, pl.ds(start, 8), :] = y[:, 128 * core : 128 * core + 128].reshape(
                radial, 8, 128
            )
        return _

    lax.fori_loop(0, 6, step, 0)


def forward_kernel(recv_ref, azimuth_ref, even_ref, odd_ref, out_ref):
    axial_parts, azimuth_parts, components = recv_ref.shape[:3]
    azimuth_count = azimuth_ref.shape[1]
    half = even_ref.shape[1]
    azimuth = (azimuth_ref[0], azimuth_ref[1])
    even = (even_ref[0], even_ref[1])
    odd = (odd_ref[0], odd_ref[1])

    def step(c, _):
        x = jnp.concatenate(
            [recv_ref[a, :, c].reshape(azimuth_count, 128) for a in range(axial_parts)], axis=1
        )
        y = table_dot(azimuth, x)
        out_ref[c, :, :half] = dot_table(y[:, :half] + y[:, half:], even, False)
        out_ref[c, :, half:] = dot_table(y[:, :half] - y[:, half:], odd, False)
        return _

    lax.fori_loop(0, components, step, 0)


def inverse(c, rhs, azimuth, even, odd, send_ref):
    half = even[0].shape[0]
    z = table_dot(azimuth, rhs)
    e = dot_table(z[:, :half], even, False)
    o = dot_table(z[:, half:], odd, True)
    for side, y in enumerate((e + o, e - o)):
        for a in range(4):
            send_ref[4 * side + a, :, c] = y[:, 128 * a : 128 * a + 128].reshape(16, 8, 128)


def total(ref):
    return ref[0] + ref[1] + ref[2]


def first_product_kernel(own_ref, other_ref, azimuth_ref, even_ref, odd_ref, send_ref, sums_ref):
    core = lax.axis_index("az") % 2
    azimuth = (azimuth_ref[core, 0], azimuth_ref[core, 1])
    even = (even_ref[0], even_ref[1])
    odd = (odd_ref[0], odd_ref[1])
    sums_ref[0] = total(own_ref)
    sums_ref[1] = total(other_ref)

    def step(c, _):
        rhs = own_ref[c] * sums_ref[1] + other_ref[c] * sums_ref[0]
        inverse(c, rhs, azimuth, even, odd, send_ref)
        return _

    lax.fori_loop(0, 3, step, 0)


def second_product_kernel(
    own_ref, other_ref, own2_ref, other2_ref, azimuth_ref, even_ref, odd_ref, send_ref, sums_ref
):
    core = lax.axis_index("az") % 2
    azimuth = (azimuth_ref[core, 0], azimuth_ref[core, 1])
    even = (even_ref[0], even_ref[1])
    odd = (odd_ref[0], odd_ref[1])
    for i, ref in enumerate((own_ref, other_ref, own2_ref, other2_ref)):
        sums_ref[i] = total(ref)

    def step(c, _):
        rhs = own_ref[c] * sums_ref[2] + own2_ref[c] * sums_ref[0]
        rhs = rhs + (other_ref[c] * sums_ref[3] + other2_ref[c] * sums_ref[1])
        inverse(c, rhs, azimuth, even, odd, send_ref)
        return _

    lax.fori_loop(0, 3, step, 0)


def gather_kernel(recv_ref, field_ref, rate_ref, tall_ref, out_ref, table_ref):
    radial = tall_ref.shape[0]
    rows = radial * 8
    lane = lax.broadcasted_iota(jnp.int32, (radial, rows), 1) % 8
    for m in range(8):
        high, low = split(jnp.where(lane == m, tall_ref[...], 0.0))
        table_ref[0, radial * m : radial * m + radial, :] = high
        table_ref[1, radial * m : radial * m + radial, :] = low
    table = (table_ref[0], table_ref[1])
    azimuth_count, axial_count = 256, 1024
    axial = lax.axis_index("ax") * 128 + lax.broadcasted_iota(jnp.int32, (1, 128), 1)
    wave = jnp.minimum(axial, axial_count - axial).astype(F32) * axial_unit
    base = rate_ref[...] + wave * wave

    def step(c, _):
        x = jnp.concatenate([recv_ref[:, core, c].reshape(rows, 128) for core in range(2)], axis=1)
        y = table_dot(table, x)
        for core in range(2):
            for i in range(8):
                m = 8 * core + i
                azimuth = lax.axis_index("az") * 16 + m
                wave_azimuth = jnp.minimum(azimuth, azimuth_count - azimuth).astype(F32)
                denom = 1.0 + viscosity * (base + wave_azimuth * wave_azimuth)
                term = y[radial * i : radial * i + radial, 128 * core : 128 * core + 128]
                out_ref[c, m] = (field_ref[c, m] + time_step * term) / denom
        return _

    lax.fori_loop(0, 3, step, 0)


def call(kernel, shape, *args, scratch=()):
    return pl.pallas_call(
        kernel,
        out_shape=jax.ShapeDtypeStruct(shape, F32),
        in_specs=[pl.BlockSpec(memory_space=pltpu.VMEM)] * len(args),
        out_specs=pl.BlockSpec(memory_space=pltpu.VMEM),
        scratch_shapes=list(scratch),
        compiler_params=pltpu.CompilerParams(vmem_limit_bytes=60 * 1024 * 1024),
    )(*args)


def body(saved_flow, saved_adjoint, tangent, second_adjoint, radial_rate):
    radial = radial_table(64)
    wide = np.tile(radial, (1, 8)).astype(np.float32)
    tall = np.repeat(radial.T, 8, axis=1).astype(np.float32)
    order = np.arange(256)
    azimuth = halves(hartley_table(order, order, 256))
    kept = [[16 * a + 8 * s + i for a in range(16) for i in range(8)] for s in range(2)]
    azimuth_back = np.stack([halves(hartley_table(np.array(rows), order, 256)) for rows in kept])
    line = np.arange(512)
    even = halves(hartley_table(line, 2 * line, 1024))
    odd = halves(hartley_table(line, 2 * line + 1, 1024))
    rate = jnp.broadcast_to(radial_rate[:, None], (64, 128))
    pairs = [(i, i ^ 1) for i in range(16)]
    table_scratch = (pltpu.VMEM((2, 512, 512), BF16),)

    def sums(count):
        return (pltpu.VMEM((count, 256, 1024), F32),)

    def spread(first, second):
        return call(spread_kernel, (64, 2, 3, 16, 128), first, second, wide, scratch=table_scratch)

    def whole(x):
        x = x.reshape((128,) + x.shape[2:])
        return lax.all_to_all(x, ("ax", "az"), 0, 0, tiled=True)

    def forward(x):
        return call(forward_kernel, (3, 256, 1024), x.reshape(8, 16, 3, 16, 128), azimuth, even, odd)

    def gather(x, field):
        return call(
            gather_kernel,
            (3, 16, 64, 128),
            x.reshape(64, 2, 3, 8, 128),
            field,
            rate,
            tall,
            scratch=table_scratch,
        )

    back = (8, 16, 3, 8, 128)
    first = whole(spread(saved_flow, tangent))
    second = whole(spread(second_adjoint, saved_adjoint))
    own = forward(first)
    other = lax.ppermute(own, "az", pairs)
    tangent_send = call(
        first_product_kernel, back, own, other, azimuth_back, even, odd, scratch=sums(2)
    )
    own2 = forward(second)
    other2 = lax.ppermute(own2, "az", pairs)
    second_send = call(
        second_product_kernel,
        back,
        own,
        other,
        own2,
        other2,
        azimuth_back,
        even,
        odd,
        scratch=sums(4),
    )
    tangent_next = gather(whole(tangent_send), tangent)
    second_next = gather(whole(second_send), second_adjoint)
    return (tangent_next, second_next)


def solution(mesh):
    spec = P(None, "az", None, "ax")
    return jax.shard_map(
        body, mesh=mesh, in_specs=(spec,) * 4 + (P(),), out_specs=(spec, spec), check_vma=False
    )
```

time: 563 us -> 203 us (0.36)
  matrix products: 207 us -> 0 us
  blocking collectives: 121 us -> 0 us
  local copies, waits for them, and re-layouts: 69.6 us -> 4.68 us
  Pallas kernels: 0 us -> 62.7 us
  other arithmetic: 34.8 us -> 0 us
  starting transfers between devices: 13.5 us -> 28.1 us
    dot_general x6 -> x0, matrix products: 207 us -> none  [the longest x2 174 us: along_axial(): jnp.einsum('nk,cmjk->cmjn', axial_table, field, precision=lax.Precision.H...]
    all_to_all x2 -> x0, blocking collectives: 121 us -> none  [the longest x1 82 us: body(): lax.all_to_all(grid, 'az', split_axis=2, concat_axis=1, tiled=True)]
    pallas_call x0 -> x8, Pallas kernels: none -> 62.7 us  [call(): pl.pallas_call(kernel, out_shape=jax.ShapeDtypeStruct(shape, F32), in_spe...]
    unnamed x12 -> x10, local copies, waits for them, and re-layouts: 25.6 us -> 3.99 us
    all_to_all x6 -> x0, local copies, waits for them, and re-layouts: 20.4 us -> none  [the longest x2 11.9 us: body(): lax.all_to_all(partial_field, 'ax', split_axis=3, concat_axis=1, tiled=True)]
    dot_general x2 -> x0, other arithmetic: 17.9 us -> none  [along_axial(): jnp.einsum('nk,cmjk->cmjn', axial_table, field, precision=lax.Precision.H...]
    transpose x3 -> x0, local copies, waits for them, and re-layouts: 14.5 us -> none  [the longest x2 10.9 us: along_azimuth(): jnp.einsum('nm,cmjk->cnjk', azimuth_table, field, precision=lax.Precision...]
    all_to_all x2 -> x4, starting transfers between devices: 13.5 us -> 25.8 us  [whole(): return lax.all_to_all(x, ('ax', 'az'), 0, 0, tiled=True)]
  transfers between devices with their start and end apart: 2 -> 6, of which waited for: 2 -> 5; matrix products, arithmetic and copies ran while one was open for 3% -> 0% of each run, Pallas kernels for 0% -> 19%
where the time goes in v1:
time: 203 us; the launch traced here: 202 us
  waiting for transfers between devices  106 us (52%)
  Pallas kernels  62.7 us (31%)
  starting transfers between devices  28.1 us (14%)
  local copies, waits for them, and re-layouts  4.68 us (2%)
    all_to_all x4, waiting for transfers between devices, whole(): return lax.all_to_all(x, ('ax', 'az'), 0, 0, tiled=True)  101 us
    pallas_call x8, Pallas kernels, call(): pl.pallas_call(kernel, out_shape=jax.ShapeDtypeStruct(shape, F32), in_spe...  62.7 us
    all_to_all x4, starting transfers between devices, whole(): return lax.all_to_all(x, ('ax', 'az'), 0, 0, tiled=True)  25.8 us
    ppermute x1, waiting for transfers between devices, body(): other2 = lax.ppermute(own2, 'az', pairs)  5.62 us
  transfers between devices with their start and end apart: 6, of which 5 were waited for; matrix products, arithmetic and copies ran while one was open for 0% of the time, Pallas kernels for 19%

profile of v1, /device:TPU:1, one launch (start us, length us, event | category | flops | bytes accessed | tf_op | source)
XLA Modules:
  0.0 202.4 jit_solution(4190144218694326351)
XLA Ops:
  0.6 7.3 %shard_map.122 = f32[64,2,3,16,128]{4,3,2,1,0:T(8,128)} custom-call(f32[3,16,64,128]{3,2,1,0:T(8,128)} %first_ref.2, f32[3,16,64,128]{3,2,1,0:T(8,128)} %field_ref.2, f32[64,512]{1,0:T(8,128)} %constant.12.clone.wide_ref), custom_call_target="tpu_custom_call" | custom-call | tf_op jit(solution)/shard_map/pallas_call | solution.py:187
  7.9 11.5 %all-to-all-start = ((f32[128,3,16,128]{3,2,1,0:T(8,128)}), f32[128,3,16,128]{3,2,1,0:T(8,128)S(1)}, u32[]{:S(2)}, u32[]{:S(2)}) async-start(f32[128,3,16,128]{3,2,1,0:T(8,128)} %bitcast.10), calls=%async_computation | async-start | bytes 6291456 | tf_op jit(solution)/shard_map/all_to_all | solution.py:220
  19.4 7.3 %shard_map.126 = f32[64,2,3,16,128]{4,3,2,1,0:T(8,128)} custom-call(f32[3,16,64,128]{3,2,1,0:T(8,128)} %field_ref.3, f32[3,16,64,128]{3,2,1,0:T(8,128)} %second_ref.3, f32[64,512]{1,0:T(8,128)} %constant.12.clone.wide_ref), custom_call_target="tpu_custom_call" | custom-call | tf_op jit(solution)/shard_map/pallas_call | solution.py:187
  26.7 34.3 %all-to-all-done = f32[128,3,16,128]{3,2,1,0:T(8,128)S(1)} async-done(((f32[128,3,16,128]{3,2,1,0:T(8,128)}), f32[128,3,16,128]{3,2,1,0:T(8,128)S(1)}, u32[]{:S(2)}, u32[]{:S(2)}) %all-to-all-start) | async-done | bytes 3145760 | tf_op jit(solution)/shard_map/all_to_all | solution.py:220
  61.0 1.7 copy-done
  62.6 5.5 %all-to-all-start.2 = ((f32[128,3,16,128]{3,2,1,0:T(8,128)}), f32[128,3,16,128]{3,2,1,0:T(8,128)}, u32[]{:S(2)}, u32[]{:S(2)}) async-start(f32[128,3,16,128]{3,2,1,0:T(8,128)} %bitcast.9), calls=%async_computation.2 | async-start | bytes 6291456 | tf_op jit(solution)/shard_map/all_to_all | solution.py:220
  68.2 8.9 %shard_map.123.own_ref = f32[3,256,1024]{2,1,0:T(8,128)} custom-call(f32[8,16,3,16,128]{4,3,2,1,0:T(8,128)} %bitcast.8, bf16[2,256,256]{2,1,0:T(8,128)(2,1)} %constant.13.clone.azimuth_ref, bf16[2,512,512]{2,1,0:T(8,128)(2,1)} %constant.14.clone.even_ref, bf16[2,512,512]{2,1,0:T(8,128)(2,1)} %constant.15.clone.odd_ref), custom_call_target="tpu_custom_call" | custom-call | tf_op jit(solution)/shard_map/pallas_call | solution.py:187
  77.1 1.3 collective-permute-start
  78.3 31.3 %all-to-all-done.2 = f32[128,3,16,128]{3,2,1,0:T(8,128)} async-done(((f32[128,3,16,128]{3,2,1,0:T(8,128)}), f32[128,3,16,128]{3,2,1,0:T(8,128)}, u32[]{:S(2)}, u32[]{:S(2)}) %all-to-all-start.2) | async-done | bytes 3145760 | tf_op jit(solution)/shard_map/all_to_all | solution.py:220
  109.6 8.9 %shard_map.127.own2_ref = f32[3,256,1024]{2,1,0:T(8,128)} custom-call(f32[8,16,3,16,128]{4,3,2,1,0:T(8,128)} %bitcast.5.recv_ref, bf16[2,256,256]{2,1,0:T(8,128)(2,1)} %constant.13.clone.azimuth_ref, bf16[2,512,512]{2,1,0:T(8,128)(2,1)} %constant.14.clone.even_ref, bf16[2,512,512]{2,1,0:T(8,128)(2,1)} %constant.15.clone.odd_ref), custom_call_target="tpu_custom_call" | custom-call | tf_op jit(solution)/shard_map/pallas_call | solution.py:187
  118.5 1.0 collective-permute-start.1
  119.6 0.0 collective-permute-done.other_ref
  119.6 5.6 %collective-permute-done.1.other2_ref = f32[3,256,1024]{2,1,0:T(8,128)} collective-permute-done((f32[3,256,1024]{2,1,0:T(8,128)}, f32[3,256,1024]{2,1,0:T(8,128)}, u32[]{:S(2)}, u32[]{:S(2)}) %collective-permute-start.1) | collective-permute-done | bytes 3145760 | tf_op jit(solution)/shard_map/ppermute | solution.py:245
  125.2 11.7 %shard_map.128 = f32[8,16,3,8,128]{4,3,2,1,0:T(8,128)} custom-call(f32[3,256,1024]{2,1,0:T(8,128)} %shard_map.123.own_ref, f32[3,256,1024]{2,1,0:T(8,128)} %copy-done.1, f32[3,256,1024]{2,1,0:T(8,128)} %shard_map.127.own2_ref, f32[3,256,1024]{2,1,0:T(8,128)} %collective-permute-done.1.other2_ref, bf16[2,2,128,256]{3,2,1,0:T(8,128)(2,1)} %constant.16.clone.azimuth_ref, ...), custom_call_target="tpu_custom_call" | custom-call | tf_op jit(solution)/shard_map/pallas_call | solution.py:187
  136.9 4.2 %all-to-all-start.3 = ((f32[128,3,8,128]{3,2,1,0:T(8,128)}), f32[128,3,8,128]{3,2,1,0:T(8,128)S(1)}, u32[]{:S(2)}, u32[]{:S(2)}) async-start(f32[128,3,8,128]{3,2,1,0:T(8,128)} %bitcast.14), calls=%async_computation.3 | async-start | bytes 3145728 | tf_op jit(solution)/shard_map/all_to_all | solution.py:220
  141.1 8.8 %shard_map.124 = f32[8,16,3,8,128]{4,3,2,1,0:T(8,128)} custom-call(f32[3,256,1024]{2,1,0:T(8,128)} %shard_map.123.own_ref, f32[3,256,1024]{2,1,0:T(8,128)} %copy-done.1, bf16[2,2,128,256]{3,2,1,0:T(8,128)(2,1)} %constant.16.clone.azimuth_ref, bf16[2,512,512]{2,1,0:T(8,128)(2,1)} %constant.14.clone.even_ref, bf16[2,512,512]{2,1,0:T(8,128)(2,1)} %constant.15.clone.odd_ref), custom_call_target="tpu_custom_call" | custom-call | tf_op jit(solution)/shard_map/pallas_call | solution.py:187
  149.8 15.8 %all-to-all-done.3 = f32[128,3,8,128]{3,2,1,0:T(8,128)S(1)} async-done(((f32[128,3,8,128]{3,2,1,0:T(8,128)}), f32[128,3,8,128]{3,2,1,0:T(8,128)S(1)}, u32[]{:S(2)}, u32[]{:S(2)}) %all-to-all-start.3) | async-done | bytes 1572896 | tf_op jit(solution)/shard_map/all_to_all | solution.py:220
  165.7 1.2 copy-done.2
  166.9 4.6 %all-to-all-start.1 = ((f32[128,3,8,128]{3,2,1,0:T(8,128)}), f32[128,3,8,128]{3,2,1,0:T(8,128)S(1)}, u32[]{:S(2)}, u32[]{:S(2)}) async-start(f32[128,3,8,128]{3,2,1,0:T(8,128)} %bitcast.11), calls=%async_computation.1 | async-start | bytes 3145728 | tf_op jit(solution)/shard_map/all_to_all | solution.py:220
  171.5 0.7 broadcast_in_dim.2.rate_ref
  172.2 5.0 %shard_map.129 = f32[3,16,64,128]{3,2,1,0:T(8,128)} custom-call(f32[64,2,3,8,128]{4,3,2,1,0:T(8,128)} %bitcast.12, f32[3,16,64,128]{3,2,1,0:T(8,128)} %field_ref.3, f32[64,128]{1,0:T(8,128)} %broadcast_in_dim.2.rate_ref, f32[64,512]{1,0:T(8,128)} %constant.17.clone.tall_ref), custom_call_target="tpu_custom_call" | custom-call | tf_op jit(solution)/shard_map/pallas_call | solution.py:187
  177.2 19.1 %all-to-all-done.1 = f32[128,3,8,128]{3,2,1,0:T(8,128)S(1)} async-done(((f32[128,3,8,128]{3,2,1,0:T(8,128)}), f32[128,3,8,128]{3,2,1,0:T(8,128)S(1)}, u32[]{:S(2)}, u32[]{:S(2)}) %all-to-all-start.1) | async-done | bytes 1572896 | tf_op jit(solution)/shard_map/all_to_all | solution.py:220
  196.2 1.2 copy-done.3
  197.4 5.0 %shard_map.125 = f32[3,16,64,128]{3,2,1,0:T(8,128)} custom-call(f32[64,2,3,8,128]{4,3,2,1,0:T(8,128)} %bitcast.13, f32[3,16,64,128]{3,2,1,0:T(8,128)} %field_ref.2, f32[64,128]{1,0:T(8,128)} %broadcast_in_dim.2.rate_ref, f32[64,512]{1,0:T(8,128)} %constant.17.clone.tall_ref), custom_call_target="tpu_custom_call" | custom-call | tf_op jit(solution)/shard_map/pallas_call | solution.py:187
  (7 shorter events, 0.0 us)
Async XLA Ops:
  7.9 53.1 %all-to-all-start = ((f32[128,3,16,128]{3,2,1,0:T(8,128)}), f32[128,3,16,128]{3,2,1,0:T(8,128)S(1)}, u32[]{:S(2)}, u32[]{:S(2)}) async-start(f32[128,3,16,128]{3,2,1,0:T(8,128)} %bitcast.10), calls=%async_computation | async-start | bytes 6291456 | tf_op jit(solution)/shard_map/all_to_all | solution.py:220
  61.0 1.7 copy-start
  62.6 47.0 %all-to-all-start.2 = ((f32[128,3,16,128]{3,2,1,0:T(8,128)}), f32[128,3,16,128]{3,2,1,0:T(8,128)}, u32[]{:S(2)}, u32[]{:S(2)}) async-start(f32[128,3,16,128]{3,2,1,0:T(8,128)} %bitcast.9), calls=%async_computation.2 | async-start | bytes 6291456 | tf_op jit(solution)/shard_map/all_to_all | solution.py:220
  77.1 42.5 %collective-permute-start = (f32[3,256,1024]{2,1,0:T(8,128)}, f32[3,256,1024]{2,1,0:T(8,128)S(1)}, u32[]{:S(2)}, u32[]{:S(2)}) collective-permute-start(f32[3,256,1024]{2,1,0:T(8,128)} %shard_map.123.own_ref), channel_id=1, source_target_pairs={{0,1},{1,0},{2,3},{3,2},{4,5},{5,4},{6,7},{7,6},{8,9},{9,8},{10,11... | collective-permute-start | bytes 9437192 | tf_op jit(solution)/shard_map/ppermute | solution.py:240
  118.5 6.7 %collective-permute-start.1 = (f32[3,256,1024]{2,1,0:T(8,128)}, f32[3,256,1024]{2,1,0:T(8,128)}, u32[]{:S(2)}, u32[]{:S(2)}) collective-permute-start(f32[3,256,1024]{2,1,0:T(8,128)} %shard_map.127.own2_ref), channel_id=1, source_target_pairs={{0,1},{1,0},{2,3},{3,2},{4,5},{5,4},{6,7},{7,6},{8,9},{9,8},{10,11... | collective-permute-start | bytes 9437192 | tf_op jit(solution)/shard_map/ppermute | solution.py:245
  119.6 5.6 %copy-start.1 = (f32[3,256,1024]{2,1,0:T(8,128)}, f32[3,256,1024]{2,1,0:T(8,128)S(1)}, u32[]{:S(2)}) copy-start(f32[3,256,1024]{2,1,0:T(8,128)S(1)} %collective-permute-done.other_ref) | copy-start | bytes 9437188
  136.9 28.8 %all-to-all-start.3 = ((f32[128,3,8,128]{3,2,1,0:T(8,128)}), f32[128,3,8,128]{3,2,1,0:T(8,128)S(1)}, u32[]{:S(2)}, u32[]{:S(2)}) async-start(f32[128,3,8,128]{3,2,1,0:T(8,128)} %bitcast.14), calls=%async_computation.3 | async-start | bytes 3145728 | tf_op jit(solution)/shard_map/all_to_all | solution.py:220
  165.7 1.2 copy-start.2
  165.7 5.8 %copy-start.4 = (f32[64]{0:T(128)S(1)}, f32[64]{0:T(128)}, u32[]{:S(2)}) copy-start(f32[64]{0:T(128)} %param.15) | copy-start | bytes 772
  166.9 29.4 %all-to-all-start.1 = ((f32[128,3,8,128]{3,2,1,0:T(8,128)}), f32[128,3,8,128]{3,2,1,0:T(8,128)S(1)}, u32[]{:S(2)}, u32[]{:S(2)}) async-start(f32[128,3,8,128]{3,2,1,0:T(8,128)} %bitcast.11), calls=%async_computation.1 | async-start | bytes 3145728 | tf_op jit(solution)/shard_map/all_to_all | solution.py:220
  196.2 1.2 copy-start.3

commit v2 on v1

--- a/solution.py
+++ b/solution.py
@@ -104,50 +104,68 @@
     lax.fori_loop(0, components, step, 0)
 
 
-def inverse(c, rhs, azimuth, even, odd, send_ref):
+def inverse(rhs, azimuth, even, odd):
     half = even[0].shape[0]
     z = table_dot(azimuth, rhs)
     e = dot_table(z[:, :half], even, False)
     o = dot_table(z[:, half:], odd, True)
-    for side, y in enumerate((e + o, e - o)):
+    return e + o, e - o
+
+
+def put(out_ref, c, sides, start):
+    for side, y in enumerate(sides):
         for a in range(4):
-            send_ref[4 * side + a, :, c] = y[:, 128 * a : 128 * a + 128].reshape(16, 8, 128)
+            block = y[start : start + 128, 128 * a : 128 * a + 128]
+            out_ref[4 * side + a, :, c] = block.reshape(16, 8, 128)
 
 
 def total(ref):
     return ref[0] + ref[1] + ref[2]
 
 
+def parts(ref):
+    return ref[0], ref[1]
+
+
 def first_product_kernel(own_ref, other_ref, azimuth_ref, even_ref, odd_ref, send_ref, sums_ref):
     core = lax.axis_index("az") % 2
-    azimuth = (azimuth_ref[core, 0], azimuth_ref[core, 1])
-    even = (even_ref[0], even_ref[1])
-    odd = (odd_ref[0], odd_ref[1])
+    azimuth = parts(azimuth_ref.at[core])
     sums_ref[0] = total(own_ref)
     sums_ref[1] = total(other_ref)
 
     def step(c, _):
         rhs = own_ref[c] * sums_ref[1] + other_ref[c] * sums_ref[0]
-        inverse(c, rhs, azimuth, even, odd, send_ref)
+        put(send_ref, c, inverse(rhs, azimuth, parts(even_ref), parts(odd_ref)), 0)
         return _
 
     lax.fori_loop(0, 3, step, 0)
 
 
-def second_product_kernel(
-    own_ref, other_ref, own2_ref, other2_ref, azimuth_ref, even_ref, odd_ref, send_ref, sums_ref
+def second_kernel(
+    recv_ref,
+    own_ref,
+    azimuth_ref,
+    back_ref,
+    even_ref,
+    odd_ref,
+    keep_ref,
+    pass_ref,
+    field_ref,
+    sums_ref,
 ):
+    forward_kernel(recv_ref, azimuth_ref, even_ref, odd_ref, field_ref)
     core = lax.axis_index("az") % 2
-    azimuth = (azimuth_ref[core, 0], azimuth_ref[core, 1])
-    even = (even_ref[0], even_ref[1])
-    odd = (odd_ref[0], odd_ref[1])
-    for i, ref in enumerate((own_ref, other_ref, own2_ref, other2_ref)):
-        sums_ref[i] = total(ref)
-
-    def step(c, _):
-        rhs = own_ref[c] * sums_ref[2] + own2_ref[c] * sums_ref[0]
-        rhs = rhs + (other_ref[c] * sums_ref[3] + other2_ref[c] * sums_ref[1])
-        inverse(c, rhs, azimuth, even, odd, send_ref)
+    sums_ref[0] = total(own_ref)
+    sums_ref[1] = total(field_ref)
+
+    def step(c, _):
+        rhs = own_ref[c] * sums_ref[1] + field_ref[c] * sums_ref[0]
+        azimuth = tuple(
+            jnp.concatenate((back_ref[core, i], back_ref[1 - core, i]), axis=0) for i in range(2)
+        )
+        sides = inverse(rhs, azimuth, parts(even_ref), parts(odd_ref))
+        put(keep_ref, c, sides, 0)
+        put(pass_ref, c, sides, 128)
         return _
 
     lax.fori_loop(0, 3, step, 0)
@@ -183,14 +201,16 @@
     lax.fori_loop(0, 3, step, 0)
 
 
-def call(kernel, shape, *args, scratch=()):
+def call(kernel, shape, *args, scratch=(), limit=16):
+    many = isinstance(shape, list)
+    vmem = pl.BlockSpec(memory_space=pltpu.VMEM)
     return pl.pallas_call(
         kernel,
-        out_shape=jax.ShapeDtypeStruct(shape, F32),
-        in_specs=[pl.BlockSpec(memory_space=pltpu.VMEM)] * len(args),
-        out_specs=pl.BlockSpec(memory_space=pltpu.VMEM),
+        out_shape=[jax.ShapeDtypeStruct(x, F32) for x in shape] if many else jax.ShapeDtypeStruct(shape, F32),
+        in_specs=[vmem] * len(args),
+        out_specs=[vmem] * len(shape) if many else vmem,
         scratch_shapes=list(scratch),
-        compiler_params=pltpu.CompilerParams(vmem_limit_bytes=60 * 1024 * 1024),
+        compiler_params=pltpu.CompilerParams(vmem_limit_bytes=limit * 1024 * 1024),
     )(*args)
 
 
@@ -209,7 +229,7 @@
     pairs = [(i, i ^ 1) for i in range(16)]
     table_scratch = (pltpu.VMEM((2, 512, 512), BF16),)
 
-    def sums(count):
+    def grid(count):
         return (pltpu.VMEM((count, 256, 1024), F32),)
 
     def spread(first, second):
@@ -219,8 +239,8 @@
         x = x.reshape((128,) + x.shape[2:])
         return lax.all_to_all(x, ("ax", "az"), 0, 0, tiled=True)
 
-    def forward(x):
-        return call(forward_kernel, (3, 256, 1024), x.reshape(8, 16, 3, 16, 128), azimuth, even, odd)
+    def planes(x):
+        return x.reshape(8, 16, 3, 16, 128)
 
     def gather(x, field):
         return call(
@@ -236,26 +256,26 @@
     back = (8, 16, 3, 8, 128)
     first = whole(spread(saved_flow, tangent))
     second = whole(spread(second_adjoint, saved_adjoint))
-    own = forward(first)
+    own = call(forward_kernel, (3, 256, 1024), planes(first), azimuth, even, odd, limit=24)
     other = lax.ppermute(own, "az", pairs)
     tangent_send = call(
-        first_product_kernel, back, own, other, azimuth_back, even, odd, scratch=sums(2)
-    )
-    own2 = forward(second)
-    other2 = lax.ppermute(own2, "az", pairs)
-    second_send = call(
-        second_product_kernel,
-        back,
+        first_product_kernel, back, own, other, azimuth_back, even, odd, scratch=grid(2), limit=24
+    )
+    tangent_back = whole(tangent_send)
+    keep, passed = call(
+        second_kernel,
+        [back, back],
+        planes(second),
         own,
-        other,
-        own2,
-        other2,
+        azimuth,
         azimuth_back,
         even,
         odd,
-        scratch=sums(4),
-    )
-    tangent_next = gather(whole(tangent_send), tangent)
+        scratch=grid(3) + grid(2),
+        limit=32,
+    )
+    second_send = keep + lax.ppermute(passed, "az", pairs)
+    tangent_next = gather(tangent_back, tangent)
     second_next = gather(whole(second_send), second_adjoint)
     return (tangent_next, second_next)
 

time: 203 us -> 196 us (0.966)
  Pallas kernels: 62.7 us -> 36.9 us
  local copies, waits for them, and re-layouts: 4.68 us -> 25.3 us
  waiting for transfers between devices: 106 us -> 102 us
    pallas_call x8 -> x7, Pallas kernels: 62.7 us -> 36.9 us  [call(): pl.pallas_call(kernel, out_shape=[jax.ShapeDtypeStruct(x, F32) for x in s...]
    unnamed x10 -> x48, local copies, waits for them, and re-layouts: 3.99 us -> 25.2 us
    ppermute x1, waiting for transfers between devices: 5.62 us -> 3.04 us  [body(): second_send = keep + lax.ppermute(passed, 'az', pairs)]
  transfers between devices with their start and end apart: 6 -> 6, of which waited for: 5 -> 5; matrix products, arithmetic and copies ran while one was open for 0% -> 1% of each run, Pallas kernels for 19% -> 15%
where the time goes in v2:
time: 196 us; the launch traced here: 195 us
  waiting for transfers between devices  102 us (52%)
  Pallas kernels  36.9 us (19%)
  starting transfers between devices  29.1 us (15%)
  local copies, waits for them, and re-layouts  25.3 us (13%)
    all_to_all x4, waiting for transfers between devices, whole(): return lax.all_to_all(x, ('ax', 'az'), 0, 0, tiled=True)  98.7 us
    pallas_call x7, Pallas kernels, call(): pl.pallas_call(kernel, out_shape=[jax.ShapeDtypeStruct(x, F32) for x in s...  36.9 us
    all_to_all x4, starting transfers between devices, whole(): return lax.all_to_all(x, ('ax', 'az'), 0, 0, tiled=True)  26.6 us
    unnamed x48, local copies, waits for them, and re-layouts  25.2 us
  transfers between devices with their start and end apart: 6, of which 5 were waited for; matrix products, arithmetic and copies ran while one was open for 1% of the time, Pallas kernels for 15%

profile of v2, /device:TPU:1, one launch (start us, length us, event | category | flops | bytes accessed | tf_op | source)
XLA Modules:
  0.0 195.2 jit_solution(2053611452932526384)
XLA Ops:
  2.0 1.4 copy-done.15
  4.4 3.7 %shard_map.122 = f32[64,2,3,16,128]{4,3,2,1,0:T(8,128)S(1)} custom-call(f32[3,16,64,128]{3,2,1,0:T(8,128)S(1)} %copy-done.15, f32[3,16,64,128]{3,2,1,0:T(8,128)S(1)} %copy-done.13, f32[64,512]{1,0:T(8,128)S(1)} %copy-done.21), custom_call_target="tpu_custom_call" | custom-call | tf_op jit(solution)/shard_map/pallas_call | solution.py:207
  8.1 1.7 copy-done.3
  9.8 11.5 %all-to-all-start = ((f32[128,3,16,128]{3,2,1,0:T(8,128)}), f32[128,3,16,128]{3,2,1,0:T(8,128)S(1)}, u32[]{:S(2)}, u32[]{:S(2)}) async-start(f32[128,3,16,128]{3,2,1,0:T(8,128)} %bitcast.10), calls=%async_computation | async-start | bytes 6291456 | tf_op jit(solution)/shard_map/all_to_all | solution.py:240
  21.3 1.4 copy-done.11
  22.7 1.4 copy-done.16
  24.1 3.7 %shard_map.126 = f32[64,2,3,16,128]{4,3,2,1,0:T(8,128)S(1)} custom-call(f32[3,16,64,128]{3,2,1,0:T(8,128)S(1)} %copy-done.11, f32[3,16,64,128]{3,2,1,0:T(8,128)S(1)} %copy-done.16, f32[64,512]{1,0:T(8,128)S(1)} %copy-done.22), custom_call_target="tpu_custom_call" | custom-call | tf_op jit(solution)/shard_map/pallas_call | solution.py:207
  27.9 1.6 copy-done.2
  29.5 33.4 %all-to-all-done = f32[128,3,16,128]{3,2,1,0:T(8,128)S(1)} async-done(((f32[128,3,16,128]{3,2,1,0:T(8,128)}), f32[128,3,16,128]{3,2,1,0:T(8,128)S(1)}, u32[]{:S(2)}, u32[]{:S(2)}) %all-to-all-start) | async-done | bytes 3145760 | tf_op jit(solution)/shard_map/all_to_all | solution.py:240
  62.9 1.7 copy-done
  64.6 5.5 %all-to-all-start.2 = ((f32[128,3,16,128]{3,2,1,0:T(8,128)}), f32[128,3,16,128]{3,2,1,0:T(8,128)}, u32[]{:S(2)}, u32[]{:S(2)}) async-start(f32[128,3,16,128]{3,2,1,0:T(8,128)} %bitcast.9), calls=%async_computation.2 | async-start | bytes 6291456 | tf_op jit(solution)/shard_map/all_to_all | solution.py:240
  70.2 1.9 copy-done.1
  75.5 4.7 %shard_map.123.own_ref = f32[3,256,1024]{2,1,0:T(8,128)S(1)} custom-call(f32[8,16,3,16,128]{4,3,2,1,0:T(8,128)S(1)} %bitcast.8, bf16[2,256,256]{2,1,0:T(8,128)(2,1)S(1)} %copy-done.18, bf16[2,512,512]{2,1,0:T(8,128)(2,1)S(1)} %copy-done.4, bf16[2,512,512]{2,1,0:T(8,128)(2,1)S(1)} %copy-done.7), custom_call_target="tpu_custom_call" | custom-call | tf_op jit(solution)/shard_map/pallas_call | solution.py:207
  81.5 30.1 %all-to-all-done.2 = f32[128,3,16,128]{3,2,1,0:T(8,128)} async-done(((f32[128,3,16,128]{3,2,1,0:T(8,128)}), f32[128,3,16,128]{3,2,1,0:T(8,128)}, u32[]{:S(2)}, u32[]{:S(2)}) %all-to-all-start.2) | async-done | bytes 3145760 | tf_op jit(solution)/shard_map/all_to_all | solution.py:240
  115.0 11.4 %shard_map.127 = (f32[8,16,3,8,128]{4,3,2,1,0:T(8,128)S(1)}, f32[8,16,3,8,128]{4,3,2,1,0:T(8,128)S(1)}) custom-call(f32[8,16,3,16,128]{4,3,2,1,0:T(8,128)} %bitcast.5.recv_ref, f32[3,256,1024]{2,1,0:T(8,128)S(1)} %shard_map.123.own_ref, bf16[2,256,256]{2,1,0:T(8,128)(2,1)S(1)} %copy-done.19, bf16[2,2,128,256]{3,2,1,0:T(8,128)(2,1)S(1)} %copy-done.17, ...), custom_call_target="tpu_custom_call" | custom-call | tf_op jit(solution)/shard_map/pallas_call | solution.py:207
  127.5 3.0 %collective-permute-done.1 = f32[8,16,3,8,128]{4,3,2,1,0:T(8,128)S(1)} collective-permute-done((f32[8,16,3,8,128]{4,3,2,1,0:T(8,128)S(1)}, f32[8,16,3,8,128]{4,3,2,1,0:T(8,128)S(1)}, u32[]{:S(2)}, u32[]{:S(2)}) %collective-permute-start.1) | collective-permute-done | bytes 1572896 | tf_op jit(solution)/shard_map/ppermute | solution.py:277
  131.9 4.8 %all-to-all-start.3 = ((f32[128,3,8,128]{3,2,1,0:T(8,128)}), f32[128,3,8,128]{3,2,1,0:T(8,128)}, u32[]{:S(2)}, u32[]{:S(2)}) async-start(f32[128,3,8,128]{3,2,1,0:T(8,128)} %bitcast.13), calls=%async_computation.3 | async-start | bytes 3145728 | tf_op jit(solution)/shard_map/all_to_all | solution.py:240
  139.2 5.9 %shard_map.124 = f32[8,16,3,8,128]{4,3,2,1,0:T(8,128)S(1)} custom-call(f32[3,256,1024]{2,1,0:T(8,128)S(1)} %shard_map.123.own_ref, f32[3,256,1024]{2,1,0:T(8,128)} %collective-permute-done.other_ref, bf16[2,2,128,256]{3,2,1,0:T(8,128)(2,1)S(1)} %copy-done.17, bf16[2,512,512]{2,1,0:T(8,128)(2,1)S(1)} %copy-done.6, bf16[2,512,512]{2,1,0:T(8,128)(2,1)S(1)} %copy-done.9), custom_call_target="tpu_custom_call" | custom-call | tf_op jit(solution)/shard_map/pallas_call | solution.py:207
  146.2 15.0 %all-to-all-done.3 = f32[128,3,8,128]{3,2,1,0:T(8,128)} async-done(((f32[128,3,8,128]{3,2,1,0:T(8,128)}), f32[128,3,8,128]{3,2,1,0:T(8,128)}, u32[]{:S(2)}, u32[]{:S(2)}) %all-to-all-start.3) | async-done | bytes 1572896 | tf_op jit(solution)/shard_map/all_to_all | solution.py:240
  161.2 4.8 %all-to-all-start.1 = ((f32[128,3,8,128]{3,2,1,0:T(8,128)}), f32[128,3,8,128]{3,2,1,0:T(8,128)S(1)}, u32[]{:S(2)}, u32[]{:S(2)}) async-start(f32[128,3,8,128]{3,2,1,0:T(8,128)} %bitcast.11), calls=%async_computation.1 | async-start | bytes 3145728 | tf_op jit(solution)/shard_map/all_to_all | solution.py:240
  166.1 4.5 %shard_map.128 = f32[3,16,64,128]{3,2,1,0:T(8,128)} custom-call(f32[64,2,3,8,128]{4,3,2,1,0:T(8,128)} %bitcast.7.recv_ref, f32[3,16,64,128]{3,2,1,0:T(8,128)S(1)} %copy-done.12, f32[64,128]{1,0:T(8,128)S(1)} %broadcast_in_dim.2.rate_ref, f32[64,512]{1,0:T(8,128)S(1)} %copy-done.20), custom_call_target="tpu_custom_call" | custom-call | tf_op jit(solution)/shard_map/pallas_call | solution.py:207
  170.6 20.2 %all-to-all-done.1 = f32[128,3,8,128]{3,2,1,0:T(8,128)S(1)} async-done(((f32[128,3,8,128]{3,2,1,0:T(8,128)}), f32[128,3,8,128]{3,2,1,0:T(8,128)S(1)}, u32[]{:S(2)}, u32[]{:S(2)}) %all-to-all-start.1) | async-done | bytes 1572896 | tf_op jit(solution)/shard_map/all_to_all | solution.py:240
  190.7 1.4 copy-done.14
  192.1 3.1 %shard_map.125 = f32[3,16,64,128]{3,2,1,0:T(8,128)} custom-call(f32[64,2,3,8,128]{4,3,2,1,0:T(8,128)S(1)} %bitcast.12, f32[3,16,64,128]{3,2,1,0:T(8,128)S(1)} %copy-done.14, f32[64,128]{1,0:T(8,128)S(1)} %broadcast_in_dim.2.rate_ref, f32[64,512]{1,0:T(8,128)S(1)} %copy-done.20), custom_call_target="tpu_custom_call" | custom-call | tf_op jit(solution)/shard_map/pallas_call | solution.py:207
  (45 shorter events, 16.7 us)
Async XLA Ops:
  0.6 1.4 copy-start.13
  2.0 1.4 copy-start.15
  8.1 1.7 copy-start.3
  9.8 11.5 %copy-start.22 = (f32[64,512]{1,0:T(8,128)S(1)}, f32[64,512]{1,0:T(8,128)}, u32[]{:S(2)}) copy-start(f32[64,512]{1,0:T(8,128)} %constant.12.clone.wide_ref) | copy-start | bytes 393220
  9.8 53.1 %all-to-all-start = ((f32[128,3,16,128]{3,2,1,0:T(8,128)}), f32[128,3,16,128]{3,2,1,0:T(8,128)S(1)}, u32[]{:S(2)}, u32[]{:S(2)}) async-start(f32[128,3,16,128]{3,2,1,0:T(8,128)} %bitcast.10), calls=%async_computation | async-start | bytes 6291456 | tf_op jit(solution)/shard_map/all_to_all | solution.py:240
  21.3 1.4 copy-start.11
  22.7 1.4 copy-start.16
  27.9 1.6 copy-start.2
  62.9 1.7 copy-start
  64.6 47.0 %all-to-all-start.2 = ((f32[128,3,16,128]{3,2,1,0:T(8,128)}), f32[128,3,16,128]{3,2,1,0:T(8,128)}, u32[]{:S(2)}, u32[]{:S(2)}) async-start(f32[128,3,16,128]{3,2,1,0:T(8,128)} %bitcast.9), calls=%async_computation.2 | async-start | bytes 6291456 | tf_op jit(solution)/shard_map/all_to_all | solution.py:240
  70.2 1.9 copy-start.1
  72.1 1.2 copy-start.4
  73.3 1.2 copy-start.7
  75.5 36.2 %copy-start.17 = (bf16[2,2,128,256]{3,2,1,0:T(8,128)(2,1)S(1)}, bf16[2,2,128,256]{3,2,1,0:T(8,128)(2,1)}, u32[]{:S(2)}) copy-start(bf16[2,2,128,256]{3,2,1,0:T(8,128)(2,1)} %constant.16.clone.azimuth_ref.back_ref) | copy-start | bytes 786436
  80.1 56.6 %collective-permute-start = (f32[3,256,1024]{2,1,0:T(8,128)S(1)}, f32[3,256,1024]{2,1,0:T(8,128)}, u32[]{:S(2)}, u32[]{:S(2)}) collective-permute-start(f32[3,256,1024]{2,1,0:T(8,128)S(1)} %shard_map.123.own_ref), channel_id=1, source_target_pairs={{0,1},{1,0},{2,3},{3,2},{4,5},{5,4},{6,7},{7,6},{8,9},{9,8},{10,11... | collective-permute-start | bytes 9437192 | tf_op jit(solution)/shard_map/ppermute | solution.py:260
  111.6 1.2 copy-start.5
  126.4 4.2 %collective-permute-start.1 = (f32[8,16,3,8,128]{4,3,2,1,0:T(8,128)S(1)}, f32[8,16,3,8,128]{4,3,2,1,0:T(8,128)S(1)}, u32[]{:S(2)}, u32[]{:S(2)}) collective-permute-start(f32[8,16,3,8,128]{4,3,2,1,0:T(8,128)S(1)} %get-tuple-element.5), channel_id=1, source_target_pairs={{0,1},{1,0},{2,3},{3,2},{4,5},{5,4},{6,7},{7,6},{8,9},{9,8},{10,11... | collective-permute-start | bytes 4718600 | tf_op jit(solution)/shard_map/ppermute | solution.py:277
  131.9 29.3 %all-to-all-start.3 = ((f32[128,3,8,128]{3,2,1,0:T(8,128)}), f32[128,3,8,128]{3,2,1,0:T(8,128)}, u32[]{:S(2)}, u32[]{:S(2)}) async-start(f32[128,3,8,128]{3,2,1,0:T(8,128)} %bitcast.13), calls=%async_computation.3 | async-start | bytes 3145728 | tf_op jit(solution)/shard_map/all_to_all | solution.py:240
  136.8 1.2 copy-start.6
  161.2 4.8 %copy-start.23 = (f32[64]{0:T(128)S(1)}, f32[64]{0:T(128)}, u32[]{:S(2)}) copy-start(f32[64]{0:T(128)} %param.15) | copy-start | bytes 772
  161.2 4.9 %copy-start.12 = (f32[3,16,64,128]{3,2,1,0:T(8,128)S(1)}, f32[3,16,64,128]{3,2,1,0:T(8,128)}, u32[]{:S(2)}) copy-start(f32[3,16,64,128]{3,2,1,0:T(8,128)} %field_ref.3) | copy-start | bytes 4718596
  161.2 4.9 %copy-start.20 = (f32[64,512]{1,0:T(8,128)S(1)}, f32[64,512]{1,0:T(8,128)}, u32[]{:S(2)}) copy-start(f32[64,512]{1,0:T(8,128)} %constant.17.clone.tall_ref) | copy-start | bytes 393220
  161.2 29.5 %all-to-all-start.1 = ((f32[128,3,8,128]{3,2,1,0:T(8,128)}), f32[128,3,8,128]{3,2,1,0:T(8,128)S(1)}, u32[]{:S(2)}, u32[]{:S(2)}) async-start(f32[128,3,8,128]{3,2,1,0:T(8,128)} %bitcast.11), calls=%async_computation.1 | async-start | bytes 3145728 | tf_op jit(solution)/shard_map/all_to_all | solution.py:240
  190.7 1.4 copy-start.14
  (6 other events, 6.4 us)

commit v3 on v2

v3 whole, which is shorter than its diff:
```python
import math

import jax
import jax.numpy as jnp
import numpy as np
from jax import lax
from jax.experimental import pallas as pl
from jax.experimental.pallas import tpu as pltpu
from jax.sharding import PartitionSpec as P

time_step = 0.1
viscosity = 0.005
axial_unit = 2.0 * math.pi / 20.0
F32 = jnp.float32
BF16 = jnp.bfloat16


def radial_table(count):
    points = np.arange(count)[:, None]
    orders = np.arange(count)[None, :]
    phases = orders * (2 * points + 1) % (4 * count)
    scales = np.where(orders == 0, math.sqrt(1.0 / count), math.sqrt(2.0 / count))
    return np.cos(phases * (math.pi / (2.0 * count))) * scales


def hartley_table(rows, cols, length):
    angles = (rows[:, None] * cols[None, :] % length) * (2.0 * math.pi / length)
    return (np.cos(angles) + np.sin(angles)) / math.sqrt(length)


def halves(table):
    table = np.asarray(table, np.float32)
    high = table.astype(BF16)
    low = (table - high.astype(np.float32)).astype(BF16)
    return np.stack((high, low))


def split(x):
    high = x.astype(BF16)
    return high, (x - high.astype(F32)).astype(BF16)


def table_dot(table, x):
    high, low = split(x)
    left = jnp.concatenate((table[0], table[0], table[1]), axis=1)
    right = jnp.concatenate((high, low, high), axis=0)
    return jnp.dot(left, right, preferred_element_type=F32)


def dot_table(x, table, turned):
    high, low = split(x)
    left = jnp.concatenate((high, low, high), axis=1)
    right = jnp.concatenate((table[0], table[0], table[1]), axis=1 if turned else 0)
    return lax.dot_general(
        left, right, (((1,), (1 if turned else 0,)), ((), ())), preferred_element_type=F32
    )


def parts(ref):
    return ref[0], ref[1]


def low_half(shape):
    return lax.broadcasted_iota(jnp.int32, shape, len(shape) - 2) % 8 < 4


def spread_kernel(flow_ref, tangent_ref, second_ref, adjoint_ref, wide_ref, out_ref, table_ref):
    fields = (flow_ref, second_ref, tangent_ref, adjoint_ref)
    radial, rows = wide_ref.shape
    low = low_half((8, rows))

    @pl.when(pl.program_id(0) == 0)
    def _():
        lane = lax.broadcasted_iota(jnp.int32, (8, rows), 1) // radial
        keep = lane == lax.broadcasted_iota(jnp.int32, (8, rows), 0) % 4
        for p in range(radial // 2):
            one = jnp.broadcast_to(wide_ref[2 * p : 2 * p + 1, :], (8, rows))
            two = jnp.broadcast_to(wide_ref[2 * p + 1 : 2 * p + 2, :], (8, rows))
            for half, (first, last) in enumerate(((one, two), (two, one))):
                pair = split(jnp.where(keep, jnp.where(low, first, last), 0.0))
                for i in range(2):
                    table_ref[half, i, 8 * p : 8 * p + 8, :] = pair[i]

    def step(group, _):
        start = pl.multiple_of(group * 8, 8)
        y = []
        for half in range(2):
            x = jnp.concatenate(
                [ref[0, pl.ds(start + 4 * half, 4)].reshape(rows, 128) for ref in fields], axis=1
            )
            y.append(table_dot(parts(table_ref.at[half]), x).reshape(radial // 2, 8, 512))
        first = low_half(y[0].shape)
        even = jnp.where(first, y[0], y[1])
        odd = pltpu.roll(jnp.where(first, y[1], y[0]), 4, 1)
        for parity, z in enumerate((even, odd)):
            for core in range(2):
                for which in range(2):
                    lane = 128 * (2 * core + which)
                    out_ref[:, parity, core, which, 0, pl.ds(start, 8), :] = z[:, :, lane : lane + 128]
        return _

    lax.fori_loop(0, 2, step, 0)


def forward(x, azimuth, axial):
    y = table_dot(azimuth, x)
    s = y[:, :512] + y[:, 512:]
    d = y[:, :512] - y[:, 512:]
    return jnp.concatenate(
        (
            dot_table(s[:, :256] + s[:, 256:], axial[0], False),
            dot_table(s[:, :256] - s[:, 256:], axial[1], False),
            dot_table(d, axial[2], False),
        ),
        axis=1,
    )


def backward(z, axial):
    a = dot_table(z[:, :256], axial[0], True)
    b = dot_table(z[:, 256:512], axial[1], True)
    o = dot_table(z[:, 512:], axial[2], True)
    e = jnp.concatenate((a + b, a - b), axis=1)
    return e + o, e - o


def plane(recv_ref, c):
    return jnp.concatenate([recv_ref[a, :, c].reshape(256, 128) for a in range(8)], axis=1)


def first_kernel(recv_ref, azimuth_ref, zero_ref, two_ref, odd_ref, out_ref):
    def step(c, _):
        axial = (parts(zero_ref), parts(two_ref), parts(odd_ref))
        out_ref[c] = forward(plane(recv_ref, c), parts(azimuth_ref), axial)
        return _

    lax.fori_loop(0, 3, step, 0)


def total(ref):
    return ref[0] + ref[1] + ref[2]


def second_kernel(
    recv_ref,
    own_ref,
    azimuth_ref,
    back_ref,
    zero_ref,
    two_ref,
    odd_ref,
    keep_ref,
    pass_ref,
    field_ref,
    sums_ref,
):
    def step(c, _):
        axial = (parts(zero_ref), parts(two_ref), parts(odd_ref))
        field_ref[c] = forward(plane(recv_ref, 3 + c), parts(azimuth_ref), axial)
        return _

    lax.fori_loop(0, 3, step, 0)
    core = lax.axis_index("az") % 2
    sums_ref[0] = total(own_ref)
    sums_ref[1] = total(field_ref)

    def product(c, _):
        rhs = own_ref[c] * sums_ref[1] + field_ref[c] * sums_ref[0]
        azimuth = tuple(
            jnp.concatenate((back_ref[core, i], back_ref[1 - core, i]), axis=0) for i in range(2)
        )
        z = table_dot(azimuth, rhs)
        keep_ref[c] = z[:128]
        pass_ref[c] = z[128:]
        return _

    lax.fori_loop(0, 3, product, 0)


def tangent_kernel(own_ref, other_ref, back_ref, out_ref, sums_ref):
    core = lax.axis_index("az") % 2
    sums_ref[0] = total(own_ref)
    sums_ref[1] = total(other_ref)

    def step(c, _):
        rhs = own_ref[c] * sums_ref[1] + other_ref[c] * sums_ref[0]
        out_ref[c] = table_dot(parts(back_ref.at[core]), rhs)
        return _

    lax.fori_loop(0, 3, step, 0)


def backward_kernel(tangent_ref, keep_ref, other_ref, zero_ref, two_ref, odd_ref, send_ref):
    axial = (parts(zero_ref), parts(two_ref), parts(odd_ref))
    for group in range(2):
        z = tangent_ref[...] if group == 0 else keep_ref[...] + other_ref[...]
        for side, y in enumerate(backward(z.reshape(384, 1024), axial)):
            for a in range(4):
                for c in range(3):
                    block = y[128 * c : 128 * c + 128, 128 * a : 128 * a + 128]
                    send_ref[4 * side + a, :, 3 * group + c] = block.reshape(16, 8, 128)


def gather_kernel(
    recv_ref, tangent_ref, second_ref, rate_ref, tall_ref, out_ref, out2_ref, table_ref, scale_ref
):
    radial, rows = tall_ref.shape[1:]
    azimuth_count, axial_count = 256, 1024

    @pl.when(pl.program_id(0) == 0)
    def _():
        lane = lax.broadcasted_iota(jnp.int32, (radial, rows), 1) % 4
        for half in range(2):
            for m in range(4):
                pair = split(jnp.where(lane == m, tall_ref[half], 0.0))
                for i in range(2):
                    table_ref[half, i, radial * m : radial * m + radial, :] = pair[i]
        axial = lax.axis_index("ax") * 128 + lax.broadcasted_iota(jnp.int32, (1, 128), 1)
        wave = jnp.minimum(axial, axial_count - axial).astype(F32) * axial_unit
        base = rate_ref[...] + wave * wave
        for m in range(16):
            azimuth = lax.axis_index("az") * 16 + m
            wave_azimuth = jnp.minimum(azimuth, azimuth_count - azimuth).astype(F32)
            scale_ref[m] = 1.0 / (1.0 + viscosity * (base + wave_azimuth * wave_azimuth))

    x = jnp.concatenate(
        [
            recv_ref[:, :, core, which, 0].reshape(32, 2, 8, 128)
            for core in range(2)
            for which in range(2)
        ],
        axis=3,
    )
    even, odd = x[:, 0], pltpu.roll(x[:, 1], 4, 1)
    first = low_half(even.shape)
    for half in range(2):
        z = jnp.where(first, even, odd) if half == 0 else jnp.where(first, odd, even)
        y = table_dot(parts(table_ref.at[half]), z.reshape(rows, 512))
        for core in range(2):
            for which, (field, out) in enumerate(((tangent_ref, out_ref), (second_ref, out2_ref))):
                lane = 128 * (2 * core + which)
                for i in range(4):
                    m = 8 * core + 4 * half + i
                    term = y[radial * i : radial * i + radial, lane : lane + 128]
                    out[0, m] = (field[0, m] + time_step * term) * scale_ref[m]


WHOLE = pl.BlockSpec(memory_space=pltpu.VMEM)


def call(kernel, shapes, *args, scratch=(), limit=24, specs=None, out_specs=None, grid=()):
    out = [jax.ShapeDtypeStruct(shape, F32) for shape in shapes]
    return pl.pallas_call(
        kernel,
        out_shape=out,
        grid=grid,
        in_specs=specs or [WHOLE] * len(args),
        out_specs=out_specs or [WHOLE] * len(out),
        scratch_shapes=list(scratch),
        compiler_params=pltpu.CompilerParams(vmem_limit_bytes=limit * 1024 * 1024),
    )(*args)


def by_component(shape, axis):
    block = shape[:axis] + (1,) + shape[axis + 1 :]
    return pl.BlockSpec(block, lambda c: tuple(c if i == axis else 0 for i in range(len(shape))))


def body(saved_flow, saved_adjoint, tangent, second_adjoint, radial_rate):
    radial = radial_table(64)
    wide = np.tile(radial, (1, 4)).astype(np.float32)
    column = np.arange(256)
    swapped = 2 * (column // 8) + 1 - column % 8 // 4
    tall = np.stack((radial.T[:, column // 4], radial.T[:, swapped])).astype(np.float32)
    order = np.arange(256)
    azimuth = halves(hartley_table(order, order, 256))
    kept = [[16 * a + 8 * s + i for a in range(16) for i in range(8)] for s in range(2)]
    back = np.stack([halves(hartley_table(np.array(rows), order, 256)) for rows in kept])
    axial = (
        halves(hartley_table(order, 4 * order, 1024)),
        halves(hartley_table(order, 4 * order + 2, 1024)),
        halves(hartley_table(np.arange(512), 2 * np.arange(512) + 1, 1024)),
    )
    rate = jnp.broadcast_to(radial_rate[:, None], (64, 128))
    pairs = [(i, i ^ 1) for i in range(16)]
    field = by_component((3, 16, 64, 128), 0)

    def swap(x):
        return lax.ppermute(x, "az", pairs)

    def whole(x):
        return lax.all_to_all(x, ("ax", "az"), 0, 0, tiled=True)

    sent = (32, 2, 2, 2, 3, 16, 128)
    (spread,) = call(
        spread_kernel,
        [sent],
        saved_flow,
        tangent,
        second_adjoint,
        saved_adjoint,
        wide,
        scratch=(pltpu.VMEM((2, 2, 256, 256), BF16),),
        specs=[field] * 4 + [pl.BlockSpec((64, 256), lambda c: (0, 0))],
        out_specs=[by_component(sent, 4)],
        grid=(3,),
    )
    recv = whole(spread.reshape(128, 6, 16, 128)).reshape(8, 16, 6, 16, 128)
    (own,) = call(first_kernel, [(3, 256, 1024)], recv, azimuth, *axial)
    other = swap(own)
    keep, passed = call(
        second_kernel,
        [(3, 128, 1024)] * 2,
        recv,
        own,
        azimuth,
        back,
        *axial,
        scratch=(pltpu.VMEM((3, 256, 1024), F32), pltpu.VMEM((2, 256, 1024), F32)),
    )
    joined = swap(passed)
    (turned,) = call(
        tangent_kernel,
        [(3, 128, 1024)],
        own,
        other,
        back,
        scratch=(pltpu.VMEM((2, 256, 1024), F32),),
    )
    (send,) = call(backward_kernel, [(8, 16, 6, 8, 128)], turned, keep, joined, *axial)
    final = (32, 2, 2, 2, 3, 8, 128)
    back_home = whole(send.reshape(128, 6, 8, 128)).reshape(final)
    shape = tangent.shape
    return tuple(
        call(
            gather_kernel,
            [shape, shape],
            back_home,
            tangent,
            second_adjoint,
            rate,
            tall,
            scratch=(pltpu.VMEM((2, 2, 256, 256), BF16), pltpu.VMEM((16, 64, 128), F32)),
            specs=[by_component(final, 4), field, field]
            + [pl.BlockSpec((64, 128), lambda c: (0, 0)), pl.BlockSpec((2, 64, 256), lambda c: (0, 0, 0))],
            out_specs=[field, field],
            grid=(3,),
        )
    )


def solution(mesh):
    spec = P(None, "az", None, "ax")
    return jax.shard_map(
        body, mesh=mesh, in_specs=(spec,) * 4 + (P(),), out_specs=(spec, spec), check_vma=False
    )
```

time: 196 us -> 165 us (0.84)
  blocking collectives: 0 us -> 132 us
  waiting for transfers between devices: 102 us -> 1.53 us
  starting transfers between devices: 29.1 us -> 1.46 us
  local copies, waits for them, and re-layouts: 25.3 us -> 6.59 us
  Pallas kernels: 36.9 us -> 22 us
    all_to_all x0 -> x2, blocking collectives: none -> 132 us  [whole(): return lax.all_to_all(x, ('ax', 'az'), 0, 0, tiled=True)]
    all_to_all x4 -> x0, waiting for transfers between devices: 98.7 us -> none  [whole(): return lax.all_to_all(x, ('ax', 'az'), 0, 0, tiled=True)]
    all_to_all x4 -> x0, starting transfers between devices: 26.6 us -> none  [whole(): return lax.all_to_all(x, ('ax', 'az'), 0, 0, tiled=True)]
    unnamed x48 -> x28, local copies, waits for them, and re-layouts: 25.2 us -> 6.52 us
    pallas_call x7 -> x6, Pallas kernels: 36.9 us -> 22 us  [call(): pl.pallas_call(kernel, out_shape=out, grid=grid, in_specs=specs or [WHOLE...]
  transfers between devices with their start and end apart: 6 -> 2, of which waited for: 5 -> 1; matrix products, arithmetic and copies ran while one was open for 1% -> 0% of each run, Pallas kernels for 15% -> 5%
where the time goes in v3:
time: 165 us; the launch traced here: 164 us
  blocking collectives  132 us (80%)
  Pallas kernels  22 us (13%)
  local copies, waits for them, and re-layouts  6.59 us (4%)
    all_to_all x2, blocking collectives, whole(): return lax.all_to_all(x, ('ax', 'az'), 0, 0, tiled=True)  132 us
    pallas_call x6, Pallas kernels, call(): pl.pallas_call(kernel, out_shape=out, grid=grid, in_specs=specs or [WHOLE...  22 us
    unnamed x28, local copies, waits for them, and re-layouts  6.52 us
  transfers between devices with their start and end apart: 2, of which 1 were waited for; matrix products, arithmetic and copies ran while one was open for 0% of the time, Pallas kernels for 5%

profile of v3, /device:TPU:1, one launch (start us, length us, event | category | flops | bytes accessed | tf_op | source)
XLA Modules:
  0.0 164.3 jit_solution(15981605710978419108)
XLA Ops:
  0.6 1.4 copy-done.1
  2.0 1.4 copy-done.3
  3.5 1.4 copy-done.7
  4.9 1.4 copy-done.8
  6.3 0.8 copy-done.12
  7.1 4.2 %shard_map.131 = f32[32,2,2,2,3,16,128]{6,5,4,3,2,1,0:T(8,128)S(1)} custom-call(f32[3,16,64,128]{3,2,1,0:T(8,128)S(1)} %copy-done.7, f32[3,16,64,128]{3,2,1,0:T(8,128)S(1)} %copy-done.1, f32[3,16,64,128]{3,2,1,0:T(8,128)S(1)} %copy-done.3, f32[3,16,64,128]{3,2,1,0:T(8,128)S(1)} %copy-done.8, f32[64,256]{1,0:T(8,128)S(1)} %copy-done.12), custom_call_target="tpu_custom_call" | custom-call | tf_op jit(solution)/shard_map/pallas_call | solution.py:253
  11.3 0.0 copy-start
  11.4 0.0 copy-start.5
  11.4 0.0 copy-start.6
  11.4 0.0 copy-start.10
  11.4 86.4 %all_to_all.10 = f32[128,6,16,128]{3,2,1,0:T(8,128)S(1)} all-to-all(f32[128,6,16,128]{3,2,1,0:T(8,128)S(1)} %bitcast.6), channel_id=1, replica_groups=mesh['ax'=8,'az'=16] {'ax','az'}, dimensions={0} | all-to-all | bytes 12582912 | tf_op jit(solution)/shard_map/all_to_all | solution.py:292
  97.8 0.0 copy-start.9
  97.8 3.9 %shard_map.132.own_ref = f32[3,256,1024]{2,1,0:T(8,128)S(1)} custom-call(f32[8,16,6,16,128]{4,3,2,1,0:T(8,128)S(1)} %bitcast.4, bf16[2,256,256]{2,1,0:T(8,128)(2,1)S(1)} %copy-done.10, bf16[2,256,256]{2,1,0:T(8,128)(2,1)S(1)} %copy-done.6, bf16[2,256,256]{2,1,0:T(8,128)(2,1)S(1)} %copy-done.5, bf16[2,512,512]{2,1,0:T(8,128)(2,1)S(1)} %copy-done), custom_call_target="tpu_custom_call" | custom-call | tf_op jit(solution)/shard_map/pallas_call | solution.py:253
  101.7 1.4 collective-permute-start
  103.1 6.3 %shard_map.134 = (f32[3,128,1024]{2,1,0:T(8,128)S(1)}, f32[3,128,1024]{2,1,0:T(8,128)S(1)}) custom-call(f32[8,16,6,16,128]{4,3,2,1,0:T(8,128)S(1)} %bitcast.5, f32[3,256,1024]{2,1,0:T(8,128)S(1)} %shard_map.132.own_ref, bf16[2,256,256]{2,1,0:T(8,128)(2,1)S(1)} %copy-done.10, bf16[2,2,128,256]{3,2,1,0:T(8,128)(2,1)S(1)} %copy-done.9, ...), custom_call_target="tpu_custom_call" | custom-call | tf_op jit(solution)/shard_map/pallas_call | solution.py:253
  109.4 0.1 collective-permute-start.1
  109.5 1.9 %shard_map.133.tangent_ref = f32[3,128,1024]{2,1,0:T(8,128)S(1)} custom-call(f32[3,256,1024]{2,1,0:T(8,128)S(1)} %shard_map.132.own_ref, f32[3,256,1024]{2,1,0:T(8,128)S(1)} %collective-permute-done.other_ref, bf16[2,2,128,256]{3,2,1,0:T(8,128)(2,1)S(1)} %copy-done.9), custom_call_target="tpu_custom_call" | custom-call | tf_op jit(solution)/shard_map/pallas_call | solution.py:253
  111.3 1.5 collective-permute-done.1.other_ref
  112.9 2.2 %shard_map.135 = f32[8,16,6,8,128]{4,3,2,1,0:T(8,128)S(1)} custom-call(f32[3,128,1024]{2,1,0:T(8,128)S(1)} %shard_map.133.tangent_ref, f32[3,128,1024]{2,1,0:T(8,128)S(1)} %get-tuple-element.4.keep_ref, f32[3,128,1024]{2,1,0:T(8,128)S(1)} %collective-permute-done.1.other_ref, bf16[2,256,256]{2,1,0:T(8,128)(2,1)S(1)} %copy-done.6, ...), custom_call_target="tpu_custom_call" | custom-call | tf_op jit(solution)/shard_map/pallas_call | solution.py:253
  115.1 0.0 copy-start.13
  115.1 0.0 copy-start.11
  115.1 45.5 %all_to_all.11 = f32[128,6,8,128]{3,2,1,0:T(8,128)S(1)} all-to-all(f32[128,6,8,128]{3,2,1,0:T(8,128)S(1)} %bitcast.8), channel_id=1, replica_groups=mesh['ax'=8,'az'=16] {'ax','az'}, dimensions={0} | all-to-all | bytes 6291456 | tf_op jit(solution)/shard_map/all_to_all | solution.py:292
  160.6 0.1 broadcast_in_dim.2.rate_ref
  160.7 3.6 %shard_map.136 = (f32[3,16,64,128]{3,2,1,0:T(8,128)}, f32[3,16,64,128]{3,2,1,0:T(8,128)}) custom-call(f32[32,2,2,2,3,8,128]{6,5,4,3,2,1,0:T(8,128)S(1)} %bitcast.7, f32[3,16,64,128]{3,2,1,0:T(8,128)S(1)} %copy-done.2, f32[3,16,64,128]{3,2,1,0:T(8,128)S(1)} %copy-done.4, f32[64,128]{1,0:T(8,128)S(1)} %broadcast_in_dim.2.rate_ref, f32[2,64,256]{2,1,0:T(8,128)S(1)} %copy-done.11), custom_call_target="tpu_custom_call" | custom-call | tf_op jit(solution)/shard_map/pallas_call | solution.py:253
  (17 shorter events, 0.0 us)
Async XLA Ops:
  0.6 1.4 copy-start.1
  2.0 1.4 copy-start.3
  3.4 1.4 copy-start.7
  4.9 1.4 copy-start.8
  6.3 0.8 copy-start.12
  11.3 86.5 %copy-start = (bf16[2,512,512]{2,1,0:T(8,128)(2,1)S(1)}, bf16[2,512,512]{2,1,0:T(8,128)(2,1)}, u32[]{:S(2)}) copy-start(bf16[2,512,512]{2,1,0:T(8,128)(2,1)} %constant.18.clone.odd_ref) | copy-start | bytes 3145732
  11.4 86.4 %copy-start.5 = (bf16[2,256,256]{2,1,0:T(8,128)(2,1)S(1)}, bf16[2,256,256]{2,1,0:T(8,128)(2,1)}, u32[]{:S(2)}) copy-start(bf16[2,256,256]{2,1,0:T(8,128)(2,1)} %constant.17.clone.two_ref) | copy-start | bytes 786436
  11.4 86.4 %copy-start.6 = (bf16[2,256,256]{2,1,0:T(8,128)(2,1)S(1)}, bf16[2,256,256]{2,1,0:T(8,128)(2,1)}, u32[]{:S(2)}) copy-start(bf16[2,256,256]{2,1,0:T(8,128)(2,1)} %constant.16.clone.zero_ref) | copy-start | bytes 786436
  11.4 86.4 %copy-start.10 = (bf16[2,256,256]{2,1,0:T(8,128)(2,1)S(1)}, bf16[2,256,256]{2,1,0:T(8,128)(2,1)}, u32[]{:S(2)}) copy-start(bf16[2,256,256]{2,1,0:T(8,128)(2,1)} %constant.15.clone.azimuth_ref) | copy-start | bytes 786436
  97.8 5.3 %copy-start.9 = (bf16[2,2,128,256]{3,2,1,0:T(8,128)(2,1)S(1)}, bf16[2,2,128,256]{3,2,1,0:T(8,128)(2,1)}, u32[]{:S(2)}) copy-start(bf16[2,2,128,256]{3,2,1,0:T(8,128)(2,1)} %constant.19.clone.back_ref) | copy-start | bytes 786436
  101.7 7.7 %collective-permute-start = (f32[3,256,1024]{2,1,0:T(8,128)S(1)}, f32[3,256,1024]{2,1,0:T(8,128)S(1)}, u32[]{:S(2)}, u32[]{:S(2)}) collective-permute-start(f32[3,256,1024]{2,1,0:T(8,128)S(1)} %shard_map.132.own_ref), channel_id=1, source_target_pairs={{0,1},{1,0},{2,3},{3,2},{4,5},{5,4},{6,7},{7,6},{8,9},{9,8},{10,11... | collective-permute-start | bytes 9437192 | tf_op jit(solution)/shard_map/ppermute | solution.py:289
  109.4 3.5 %collective-permute-start.1 = (f32[3,128,1024]{2,1,0:T(8,128)S(1)}, f32[3,128,1024]{2,1,0:T(8,128)S(1)}, u32[]{:S(2)}, u32[]{:S(2)}) collective-permute-start(f32[3,128,1024]{2,1,0:T(8,128)S(1)} %get-tuple-element.5), channel_id=1, source_target_pairs={{0,1},{1,0},{2,3},{3,2},{4,5},{5,4},{6,7},{7,6},{8,9},{9,8},{10,11... | collective-permute-start | bytes 4718600 | tf_op jit(solution)/shard_map/ppermute | solution.py:289
  115.1 45.5 %copy-start.13 = (f32[64]{0:T(128)S(1)}, f32[64]{0:T(128)}, u32[]{:S(2)}) copy-start(f32[64]{0:T(128)} %param.16) | copy-start | bytes 772
  115.1 45.6 %copy-start.2 = (f32[3,16,64,128]{3,2,1,0:T(8,128)S(1)}, f32[3,16,64,128]{3,2,1,0:T(8,128)}, u32[]{:S(2)}) copy-start(f32[3,16,64,128]{3,2,1,0:T(8,128)} %tangent_ref.3) | copy-start | bytes 4718596
  115.1 45.6 %copy-start.4 = (f32[3,16,64,128]{3,2,1,0:T(8,128)S(1)}, f32[3,16,64,128]{3,2,1,0:T(8,128)}, u32[]{:S(2)}) copy-start(f32[3,16,64,128]{3,2,1,0:T(8,128)} %second_ref.3) | copy-start | bytes 4718596
  115.1 45.6 %copy-start.11 = (f32[2,64,256]{2,1,0:T(8,128)S(1)}, f32[2,64,256]{2,1,0:T(8,128)}, u32[]{:S(2)}) copy-start(f32[2,64,256]{2,1,0:T(8,128)} %constant.20.clone.tall_ref) | copy-start | bytes 393220

commit v4 on v3

v4 whole, which is shorter than its diff:
```python
import math

import jax
import jax.numpy as jnp
import numpy as np
from jax import lax
from jax.experimental import pallas as pl
from jax.experimental.pallas import tpu as pltpu
from jax.sharding import PartitionSpec as P

time_step = 0.1
viscosity = 0.005
axial_unit = 2.0 * math.pi / 20.0
F32 = jnp.float32
BF16 = jnp.bfloat16


def radial_table(count):
    points = np.arange(count)[:, None]
    orders = np.arange(count)[None, :]
    phases = orders * (2 * points + 1) % (4 * count)
    scales = np.where(orders == 0, math.sqrt(1.0 / count), math.sqrt(2.0 / count))
    return np.cos(phases * (math.pi / (2.0 * count))) * scales


def hartley_table(rows, cols, length):
    angles = (rows[:, None] * cols[None, :] % length) * (2.0 * math.pi / length)
    return (np.cos(angles) + np.sin(angles)) / math.sqrt(length)


def halves(table):
    table = np.asarray(table, np.float32)
    high = table.astype(BF16)
    low = (table - high.astype(np.float32)).astype(BF16)
    return np.stack((high, low))


def split(x):
    high = x.astype(BF16)
    return high, (x - high.astype(F32)).astype(BF16)


def table_dot(table, x):
    high, low = split(x)
    left = jnp.concatenate((table[0], table[0], table[1]), axis=1)
    right = jnp.concatenate((high, low, high), axis=0)
    return jnp.dot(left, right, preferred_element_type=F32)


def dot_table(x, table, turned):
    high, low = split(x)
    left = jnp.concatenate((high, low, high), axis=1)
    right = jnp.concatenate((table[0], table[0], table[1]), axis=1 if turned else 0)
    return lax.dot_general(
        left, right, (((1,), (1 if turned else 0,)), ((), ())), preferred_element_type=F32
    )


def parts(ref):
    return ref[0], ref[1]


def low_half(shape):
    return lax.broadcasted_iota(jnp.int32, shape, len(shape) - 2) % 8 < 4


def spread_kernel(
    flow_ref, tangent_ref, second_ref, adjoint_ref, wide_ref, out_ref, table_ref, field_ref, sems
):
    radial, rows = wide_ref.shape

    def fetch(i, ref, step):
        c, start = step // 2, pl.multiple_of(step % 2 * 8, 8)
        place = (c, pl.ds(start, 8))
        return pltpu.make_async_copy(ref.at[place], field_ref.at[(i, *place)], sems.at[i, step])

    fields = tuple(enumerate((flow_ref, second_ref, tangent_ref, adjoint_ref)))
    for step in range(6):
        for i, ref in fields:
            fetch(i, ref, step).start()
    low = low_half((8, rows))
    lane = lax.broadcasted_iota(jnp.int32, (8, rows), 1) // radial
    keep = lane == lax.broadcasted_iota(jnp.int32, (8, rows), 0) % 4
    for p in range(radial // 2):
        one = jnp.broadcast_to(wide_ref[2 * p : 2 * p + 1, :], (8, rows))
        two = jnp.broadcast_to(wide_ref[2 * p + 1 : 2 * p + 2, :], (8, rows))
        for half, (first, last) in enumerate(((one, two), (two, one))):
            pair = split(jnp.where(keep, jnp.where(low, first, last), 0.0))
            for i in range(2):
                table_ref[half, i, 8 * p : 8 * p + 8, :] = pair[i]

    def work(step, _):
        for i, ref in fields:
            fetch(i, ref, step).wait()
        c, start = step // 2, pl.multiple_of(step % 2 * 8, 8)
        y = []
        for half in range(2):
            x = jnp.concatenate(
                [field_ref[i, c, pl.ds(start + 4 * half, 4)].reshape(rows, 128) for i in range(4)],
                axis=1,
            )
            y.append(table_dot(parts(table_ref.at[half]), x).reshape(radial // 2, 8, 512))
        first = low_half(y[0].shape)
        even = jnp.where(first, y[0], y[1])
        odd = pltpu.roll(jnp.where(first, y[1], y[0]), 4, 1)
        for parity, z in enumerate((even, odd)):
            for core in range(2):
                for which in range(2):
                    lane = 128 * (2 * core + which)
                    out_ref[:, parity, core, which, c, pl.ds(start, 8), :] = z[:, :, lane : lane + 128]
        return _

    lax.fori_loop(0, 6, work, 0)


def forward(x, azimuth, axial):
    y = jnp.concatenate(
        (table_dot(azimuth[0], x[:128] + x[128:]), table_dot(azimuth[1], x[:128] - x[128:])), axis=0
    )
    s = y[:, :512] + y[:, 512:]
    d = y[:, :512] - y[:, 512:]
    return jnp.concatenate(
        (
            dot_table(s[:, :256] + s[:, 256:], axial[0], False),
            dot_table(s[:, :256] - s[:, 256:], axial[1], False),
            dot_table(d, axial[2], False),
        ),
        axis=1,
    )


def backward(z, axial):
    a = dot_table(z[:, :256], axial[0], True)
    b = dot_table(z[:, 256:512], axial[1], True)
    o = dot_table(z[:, 512:], axial[2], True)
    e = jnp.concatenate((a + b, a - b), axis=1)
    return e + o, e - o


def plane(recv_ref, c):
    return jnp.concatenate([recv_ref[a, :, c].reshape(256, 128) for a in range(8)], axis=1)


def put(z, axial, send_ref, group):
    for side, y in enumerate(backward(z, axial)):
        for a in range(4):
            for c in range(3):
                block = y[128 * c : 128 * c + 128, 128 * a : 128 * a + 128]
                send_ref[4 * side + a, :, 3 * group + c] = block.reshape(16, 8, 128)


def add_to(sum_ref, c, value):
    sum_ref[...] = jnp.where(c == 0, 0.0, sum_ref[...]) + value


def first_kernel(recv_ref, azimuth_ref, zero_ref, two_ref, odd_ref, out_ref, sum_ref):
    def step(c, _):
        axial = (parts(zero_ref), parts(two_ref), parts(odd_ref))
        azimuth = (parts(azimuth_ref.at[0]), parts(azimuth_ref.at[1]))
        y = forward(plane(recv_ref, c), azimuth, axial)
        out_ref[c] = y
        add_to(sum_ref, c, y)
        return _

    lax.fori_loop(0, 3, step, 0)


def second_kernel(
    recv_ref,
    own_ref,
    own_sum_ref,
    azimuth_ref,
    back_ref,
    zero_ref,
    two_ref,
    odd_ref,
    keep_ref,
    pass_ref,
    field_ref,
    sum_ref,
):
    def step(c, _):
        axial = (parts(zero_ref), parts(two_ref), parts(odd_ref))
        azimuth = (parts(azimuth_ref.at[0]), parts(azimuth_ref.at[1]))
        y = forward(plane(recv_ref, 3 + c), azimuth, axial)
        field_ref[c] = y
        add_to(sum_ref, c, y)
        return _

    lax.fori_loop(0, 3, step, 0)
    core = lax.axis_index("az") % 2

    def product(c, _):
        rhs = own_ref[c] * sum_ref[...] + field_ref[c] * own_sum_ref[...]
        side = []
        for parity in range(2):
            table = tuple(
                jnp.concatenate((back_ref[core, parity, i], back_ref[1 - core, parity, i]), axis=0)
                for i in range(2)
            )
            side.append(table_dot(table, rhs[128 * parity : 128 * parity + 128]))
        upper, lower = side[0] + side[1], side[0] - side[1]
        keep_ref[c] = jnp.concatenate((upper[:64], lower[:64]), axis=0)
        pass_ref[c] = jnp.concatenate((upper[64:], lower[64:]), axis=0)
        return _

    lax.fori_loop(0, 3, product, 0)


def tangent_kernel(
    own_ref,
    own_sum_ref,
    other_ref,
    back_ref,
    zero_ref,
    two_ref,
    odd_ref,
    send_ref,
    sum_ref,
    turned_ref,
):
    core = lax.axis_index("az") % 2
    sum_ref[...] = other_ref[0] + other_ref[1] + other_ref[2]

    def step(c, _):
        rhs = own_ref[c] * sum_ref[...] + other_ref[c] * own_sum_ref[...]
        e = table_dot(parts(back_ref.at[core, 0]), rhs[:128])
        o = table_dot(parts(back_ref.at[core, 1]), rhs[128:])
        turned_ref[c] = jnp.concatenate((e + o, e - o), axis=0)
        return _

    lax.fori_loop(0, 3, step, 0)
    axial = (parts(zero_ref), parts(two_ref), parts(odd_ref))
    put(turned_ref[...].reshape(384, 1024), axial, send_ref, 0)


def join_kernel(tangent_ref, keep_ref, other_ref, zero_ref, two_ref, odd_ref, send_ref):
    send_ref[:, :, :3] = tangent_ref[...]
    z = keep_ref[...] + other_ref[...]
    put(z.reshape(384, 1024), (parts(zero_ref), parts(two_ref), parts(odd_ref)), send_ref, 1)


def gather_kernel(
    recv_ref, tangent_ref, second_ref, rate_ref, table_ref, out_ref, out2_ref, result_ref, scale_ref, sems
):
    radial = rate_ref.shape[0]
    azimuth_count, axial_count = 256, 1024
    axial = lax.axis_index("ax") * 128 + lax.broadcasted_iota(jnp.int32, (1, 128), 1)
    wave = jnp.minimum(axial, axial_count - axial).astype(F32) * axial_unit
    base = rate_ref[...] + wave * wave

    def scale(m, _):
        azimuth = lax.axis_index("az") * 16 + m
        wave_azimuth = jnp.minimum(azimuth, azimuth_count - azimuth).astype(F32)
        scale_ref[m] = 1.0 / (1.0 + viscosity * (base + wave_azimuth * wave_azimuth))
        return _

    lax.fori_loop(0, 16, scale, 0)
    outs = (out_ref, out2_ref)
    fields = (tangent_ref, second_ref)

    def give(which, c, core):
        place = (c, pl.ds(8 * core, 8))
        return pltpu.make_async_copy(
            result_ref.at[(which, *place)], outs[which].at[place], sems.at[which, c, core]
        )

    def step(c, _):
        x = jnp.concatenate(
            [recv_ref[:, :, core, which, c] for core in range(2) for which in range(2)], axis=3
        )
        even, odd = x[:, 0], pltpu.roll(x[:, 1], 4, 1)
        first = low_half(even.shape)
        for half in range(2):
            z = jnp.where(first, even, odd) if half == 0 else jnp.where(first, odd, even)
            y = table_dot(parts(table_ref.at[half]), z.reshape(4 * radial, 512))
            for core in range(2):
                for which in range(2):
                    lane = 128 * (2 * core + which)
                    for i in range(4):
                        m = 8 * core + 4 * half + i
                        term = y[radial * i : radial * i + radial, lane : lane + 128]
                        result_ref[which, c, m] = (fields[which][c, m] + time_step * term) * scale_ref[m]
        for which in range(2):
            for core in range(2):
                give(which, c, core).start()
        return _

    lax.fori_loop(0, 3, step, 0)

    def finish(c, _):
        for which in range(2):
            for core in range(2):
                give(which, c, core).wait()
        return _

    lax.fori_loop(0, 3, finish, 0)


WHOLE = pl.BlockSpec(memory_space=pltpu.VMEM)
LEFT = pl.BlockSpec(memory_space=pl.ANY)


def call(kernel, shapes, *args, scratch=(), limit=24, specs=None, out_spec=WHOLE):
    out = [jax.ShapeDtypeStruct(shape, F32) for shape in shapes]
    return pl.pallas_call(
        kernel,
        out_shape=out,
        in_specs=specs or [WHOLE] * len(args),
        out_specs=[out_spec] * len(out),
        scratch_shapes=list(scratch),
        compiler_params=pltpu.CompilerParams(vmem_limit_bytes=limit * 1024 * 1024),
    )(*args)


def gather_table(radial):
    column = np.arange(256)
    swapped = 2 * (column // 8) + 1 - column % 8 // 4
    sides = []
    for j in (column // 4, swapped):
        keep = np.arange(4)[:, None, None] == (column % 4)[None, None, :]
        sides.append(halves(np.where(keep, radial.T[:, j][None], 0.0).reshape(256, 256)))
    return np.stack(sides)


def body(saved_flow, saved_adjoint, tangent, second_adjoint, radial_rate):
    radial = radial_table(64)
    wide = np.tile(radial, (1, 4)).astype(np.float32)
    half, quarter = np.arange(128), np.arange(256)
    azimuth = np.stack([halves(hartley_table(2 * half + p, half, 256)) for p in range(2)])
    kept = [np.array([16 * a + 8 * s + i for a in range(8) for i in range(8)]) for s in range(2)]
    back = np.stack(
        [
            np.stack([halves(hartley_table(rows, 2 * half + p, 256)) for p in range(2)])
            for rows in kept
        ]
    )
    axial = (
        halves(hartley_table(quarter, 4 * quarter, 1024)),
        halves(hartley_table(quarter, 4 * quarter + 2, 1024)),
        halves(hartley_table(np.arange(512), 2 * np.arange(512) + 1, 1024)),
    )
    rate = jnp.broadcast_to(radial_rate[:, None], (64, 128))
    pairs = [(i, i ^ 1) for i in range(16)]
    grid, rows = (256, 1024), (128, 1024)

    def swap(x):
        return lax.ppermute(x, "az", pairs)

    def whole(x):
        return lax.all_to_all(x, ("ax", "az"), 0, 0, tiled=True)

    (spread,) = call(
        spread_kernel,
        [(32, 2, 2, 2, 3, 16, 128)],
        *(
            pltpu.with_memory_space_constraint(x, pltpu.HBM)
            for x in (saved_flow, tangent, second_adjoint, saved_adjoint)
        ),
        wide,
        scratch=(
            pltpu.VMEM((2, 2, 256, 256), BF16),
            pltpu.VMEM((4, 3, 16, 64, 128), F32),
            pltpu.SemaphoreType.DMA((4, 6)),
        ),
        specs=[LEFT] * 4 + [WHOLE],
    )
    recv = whole(spread.reshape(128, 6, 16, 128)).reshape(8, 16, 6, 16, 128)
    own, own_sum = call(first_kernel, [(3, *grid), grid], recv, azimuth, *axial)
    other = swap(own)
    keep, passed = call(
        second_kernel,
        [(3, *rows)] * 2,
        recv,
        own,
        own_sum,
        azimuth,
        back,
        *axial,
        scratch=(pltpu.VMEM((3, *grid), F32), pltpu.VMEM(grid, F32)),
    )
    joined = swap(passed)
    (turned,) = call(
        tangent_kernel,
        [(8, 16, 3, 8, 128)],
        own,
        own_sum,
        other,
        back,
        *axial,
        scratch=(pltpu.VMEM(grid, F32), pltpu.VMEM((3, *rows), F32)),
    )
    (send,) = call(join_kernel, [(8, 16, 6, 8, 128)], turned, keep, joined, *axial)
    home = whole(send.reshape(128, 6, 8, 128)).reshape(32, 2, 2, 2, 3, 8, 128)
    shape = tangent.shape
    return tuple(
        call(
            gather_kernel,
            [shape, shape],
            home,
            tangent,
            second_adjoint,
            rate,
            gather_table(radial),
            scratch=(
                pltpu.VMEM((2, *shape), F32),
                pltpu.VMEM(shape[1:], F32),
                pltpu.SemaphoreType.DMA((2, 3, 2)),
            ),
            out_spec=LEFT,
        )
    )


def solution(mesh):
    spec = P(None, "az", None, "ax")
    return jax.shard_map(
        body, mesh=mesh, in_specs=(spec,) * 4 + (P(),), out_specs=(spec, spec), check_vma=False
    )
```

time: 165 us -> 157 us (0.952)
  local copies, waits for them, and re-layouts: 6.59 us -> 0.97 us
    unnamed x28 -> x20, local copies, waits for them, and re-layouts: 6.52 us -> 0.9 us
where the time goes in v4:
time: 157 us
  blocking collectives  132 us (84%)
  Pallas kernels  21.4 us (14%)
    all_to_all x2, blocking collectives, whole(): return lax.all_to_all(x, ('ax', 'az'), 0, 0, tiled=True)  132 us
    pallas_call x6, Pallas kernels, call(): pl.pallas_call(kernel, out_shape=out, in_specs=specs or [WHOLE] * len(arg...  21.4 us
  transfers between devices with their start and end apart: 2, of which 1 were waited for; matrix products, arithmetic and copies ran while one was open for 0% of the time, Pallas kernels for 5%

profile of v4, /device:TPU:1, one launch (start us, length us, event | category | flops | bytes accessed | tf_op | source)
XLA Modules:
  0.0 157.0 jit_solution(8722645632996646773)
XLA Ops:
  0.6 0.0 copy-start.8
  0.6 0.8 copy-done.8
  1.5 5.0 %shard_map.131 = f32[32,2,2,2,3,16,128]{6,5,4,3,2,1,0:T(8,128)S(1)} custom-call(f32[3,16,64,128]{3,2,1,0:T(8,128)} %flow_ref.1, f32[3,16,64,128]{3,2,1,0:T(8,128)} %tangent_ref.3, f32[3,16,64,128]{3,2,1,0:T(8,128)} %second_ref.3, f32[3,16,64,128]{3,2,1,0:T(8,128)} %adjoint_ref.1, f32[64,256]{1,0:T(8,128)S(1)} %copy-done.8), custom_call_target="tpu_custom_call" | custom-call | tf_op jit(solution)/shard_map/pallas_call | solution.py:306
  6.5 0.0 copy-start
  6.5 0.0 copy-start.3
  6.5 0.0 copy-start.4
  6.6 0.0 copy-start.5
  6.6 86.4 %all_to_all.10 = f32[128,6,16,128]{3,2,1,0:T(8,128)S(1)} all-to-all(f32[128,6,16,128]{3,2,1,0:T(8,128)S(1)} %bitcast.6), channel_id=1, replica_groups=mesh['ax'=8,'az'=16] {'ax','az'}, dimensions={0} | all-to-all | bytes 12582912 | tf_op jit(solution)/shard_map/all_to_all | solution.py:351
  93.0 0.0 copy-start.6
  93.0 3.7 %shard_map.132 = (f32[3,256,1024]{2,1,0:T(8,128)S(1)}, f32[256,1024]{1,0:T(8,128)S(1)}) custom-call(f32[8,16,6,16,128]{4,3,2,1,0:T(8,128)S(1)} %bitcast.4, bf16[2,2,128,128]{3,2,1,0:T(8,128)(2,1)S(1)} %copy-done.5, bf16[2,256,256]{2,1,0:T(8,128)(2,1)S(1)} %copy-done.4, bf16[2,256,256]{2,1,0:T(8,128)(2,1)S(1)} %copy-done.3, bf16[2,512,512]{2,1,0:T(8,128)(2,1)S(1)} %copy-done), custom_call_target="tpu_custom_call" | custom-call | tf_op jit(solution)/shard_map/pallas_call | solution.py:306
  96.7 1.3 collective-permute-start
  98.1 5.3 %shard_map.134 = (f32[3,128,1024]{2,1,0:T(8,128)S(1)}, f32[3,128,1024]{2,1,0:T(8,128)S(1)}) custom-call(f32[8,16,6,16,128]{4,3,2,1,0:T(8,128)S(1)} %bitcast.5, f32[3,256,1024]{2,1,0:T(8,128)S(1)} %get-tuple-element.6.own_ref, f32[256,1024]{1,0:T(8,128)S(1)} %get-tuple-element.7.own_sum_ref, bf16[2,2,128,128]{3,2,1,0:T(8,128)(2,1)S(1)} %copy-done.5, ...), custom_call_target="tpu_custom_call" | custom-call | tf_op jit(solution)/shard_map/pallas_call | solution.py:306
  103.4 0.1 collective-permute-start.1
  103.4 0.0 collective-permute-done.other_ref
  103.5 2.8 %shard_map.133.tangent_ref = f32[8,16,3,8,128]{4,3,2,1,0:T(8,128)S(1)} custom-call(f32[3,256,1024]{2,1,0:T(8,128)S(1)} %get-tuple-element.6.own_ref, f32[256,1024]{1,0:T(8,128)S(1)} %get-tuple-element.7.own_sum_ref, f32[3,256,1024]{2,1,0:T(8,128)S(1)} %collective-permute-done.other_ref, bf16[2,2,2,64,128]{4,3,2,1,0:T(8,128)(2,1)S(1)} %copy-done.6, ...), custom_call_target="tpu_custom_call" | custom-call | tf_op jit(solution)/shard_map/pallas_call | solution.py:306
  106.2 0.6 collective-permute-done.1.other_ref
  106.8 1.2 shard_map.135
  108.0 0.0 copy-start.9
  108.1 0.0 copy-start.1
  108.1 0.0 copy-start.2
  108.1 0.0 copy-start.7
  108.1 45.5 %all_to_all.11 = f32[128,6,8,128]{3,2,1,0:T(8,128)S(1)} all-to-all(f32[128,6,8,128]{3,2,1,0:T(8,128)S(1)} %bitcast.7), channel_id=1, replica_groups=mesh['ax'=8,'az'=16] {'ax','az'}, dimensions={0} | all-to-all | bytes 6291456 | tf_op jit(solution)/shard_map/all_to_all | solution.py:351
  153.5 0.1 broadcast_in_dim.2.rate_ref
  153.6 3.4 %shard_map.136 = (f32[3,16,64,128]{3,2,1,0:T(8,128)}, f32[3,16,64,128]{3,2,1,0:T(8,128)}) custom-call(f32[32,2,2,2,3,8,128]{6,5,4,3,2,1,0:T(8,128)S(1)} %bitcast.8, f32[3,16,64,128]{3,2,1,0:T(8,128)S(1)} %copy-done.1, f32[3,16,64,128]{3,2,1,0:T(8,128)S(1)} %copy-done.2, f32[64,128]{1,0:T(8,128)S(1)} %broadcast_in_dim.2.rate_ref, ...), custom_call_target="tpu_custom_call" | custom-call | tf_op jit(solution)/shard_map/pallas_call | solution.py:306
  (9 shorter events, 0.0 us)
Async XLA Ops:
  0.6 0.8 copy-start.8
  6.5 86.4 %copy-start = (bf16[2,512,512]{2,1,0:T(8,128)(2,1)S(1)}, bf16[2,512,512]{2,1,0:T(8,128)(2,1)}, u32[]{:S(2)}) copy-start(bf16[2,512,512]{2,1,0:T(8,128)(2,1)} %constant.18.clone.odd_ref) | copy-start | bytes 3145732
  6.5 86.4 %copy-start.3 = (bf16[2,256,256]{2,1,0:T(8,128)(2,1)S(1)}, bf16[2,256,256]{2,1,0:T(8,128)(2,1)}, u32[]{:S(2)}) copy-start(bf16[2,256,256]{2,1,0:T(8,128)(2,1)} %constant.17.clone.two_ref) | copy-start | bytes 786436
  6.5 86.4 %copy-start.4 = (bf16[2,256,256]{2,1,0:T(8,128)(2,1)S(1)}, bf16[2,256,256]{2,1,0:T(8,128)(2,1)}, u32[]{:S(2)}) copy-start(bf16[2,256,256]{2,1,0:T(8,128)(2,1)} %constant.16.clone.zero_ref) | copy-start | bytes 786436
  6.6 86.4 %copy-start.5 = (bf16[2,2,128,128]{3,2,1,0:T(8,128)(2,1)S(1)}, bf16[2,2,128,128]{3,2,1,0:T(8,128)(2,1)}, u32[]{:S(2)}) copy-start(bf16[2,2,128,128]{3,2,1,0:T(8,128)(2,1)} %constant.15.clone.azimuth_ref) | copy-start | bytes 393220
  93.0 5.1 %copy-start.6 = (bf16[2,2,2,64,128]{4,3,2,1,0:T(8,128)(2,1)S(1)}, bf16[2,2,2,64,128]{4,3,2,1,0:T(8,128)(2,1)}, u32[]{:S(2)}) copy-start(bf16[2,2,2,64,128]{4,3,2,1,0:T(8,128)(2,1)} %constant.19.clone.back_ref) | copy-start | bytes 393220
  96.7 6.7 %collective-permute-start = (f32[3,256,1024]{2,1,0:T(8,128)S(1)}, f32[3,256,1024]{2,1,0:T(8,128)S(1)}, u32[]{:S(2)}, u32[]{:S(2)}) collective-permute-start(f32[3,256,1024]{2,1,0:T(8,128)S(1)} %get-tuple-element.6.own_ref), channel_id=1, source_target_pairs={{0,1},{1,0},{2,3},{3,2},{4,5},{5,4},{6,7},{7,6},{8,9},{9,8},{10,11... | collective-permute-start | bytes 9437192 | tf_op jit(solution)/shard_map/ppermute | solution.py:348
  103.4 3.5 %collective-permute-start.1 = (f32[3,128,1024]{2,1,0:T(8,128)S(1)}, f32[3,128,1024]{2,1,0:T(8,128)S(1)}, u32[]{:S(2)}, u32[]{:S(2)}) collective-permute-start(f32[3,128,1024]{2,1,0:T(8,128)S(1)} %get-tuple-element.9), channel_id=1, source_target_pairs={{0,1},{1,0},{2,3},{3,2},{4,5},{5,4},{6,7},{7,6},{8,9},{9,8},{10,11... | collective-permute-start | bytes 4718600 | tf_op jit(solution)/shard_map/ppermute | solution.py:348
  108.0 45.5 %copy-start.9 = (f32[64]{0:T(128)S(1)}, f32[64]{0:T(128)}, u32[]{:S(2)}) copy-start(f32[64]{0:T(128)} %param.16) | copy-start | bytes 772
  108.1 45.6 %copy-start.1 = (f32[3,16,64,128]{3,2,1,0:T(8,128)S(1)}, f32[3,16,64,128]{3,2,1,0:T(8,128)}, u32[]{:S(2)}) copy-start(f32[3,16,64,128]{3,2,1,0:T(8,128)} %tangent_ref.3) | copy-start | bytes 4718596
  108.1 45.6 %copy-start.2 = (f32[3,16,64,128]{3,2,1,0:T(8,128)S(1)}, f32[3,16,64,128]{3,2,1,0:T(8,128)}, u32[]{:S(2)}) copy-start(f32[3,16,64,128]{3,2,1,0:T(8,128)} %second_ref.3) | copy-start | bytes 4718596
  108.1 45.6 %copy-start.7 = (bf16[2,2,256,256]{3,2,1,0:T(8,128)(2,1)S(1)}, bf16[2,2,256,256]{3,2,1,0:T(8,128)(2,1)}, u32[]{:S(2)}) copy-start(bf16[2,2,256,256]{3,2,1,0:T(8,128)(2,1)} %constant.20.clone.table_ref) | copy-start | bytes 1572868

commit v5 on v4

--- a/solution.py
+++ b/solution.py
@@ -40,11 +40,15 @@
     return high, (x - high.astype(F32)).astype(BF16)
 
 
+def stacked(table):
+    high, low = halves(table)
+    return np.block([[high, high], [low, np.zeros_like(low)]])
+
+
 def table_dot(table, x):
-    high, low = split(x)
-    left = jnp.concatenate((table[0], table[0], table[1]), axis=1)
-    right = jnp.concatenate((high, low, high), axis=0)
-    return jnp.dot(left, right, preferred_element_type=F32)
+    out = jnp.dot(table, jnp.concatenate(split(x), axis=0), preferred_element_type=F32)
+    half = out.shape[0] // 2
+    return out[:half] + out[half:]
 
 
 def dot_table(x, table, turned):
@@ -60,14 +64,27 @@
     return ref[0], ref[1]
 
 
-def low_half(shape):
-    return lax.broadcasted_iota(jnp.int32, shape, len(shape) - 2) % 8 < 4
+def pick(arrays, first, step):
+    block = lax.broadcasted_iota(jnp.int32, arrays[0].shape, 1) // 2
+    out = arrays[first % 4]
+    for b in range(1, 4):
+        out = jnp.where(block == b, arrays[(first + step * b) % 4], out)
+    return out
 
 
 def spread_kernel(
-    flow_ref, tangent_ref, second_ref, adjoint_ref, wide_ref, out_ref, table_ref, field_ref, sems
+    flow_ref,
+    tangent_ref,
+    second_ref,
+    adjoint_ref,
+    radial_ref,
+    out_ref,
+    table_ref,
+    field_ref,
+    sem,
+    sems,
 ):
-    radial, rows = wide_ref.shape
+    fetch_table = pltpu.make_async_copy(radial_ref, table_ref, sem)
 
     def fetch(i, ref, step):
         c, start = step // 2, pl.multiple_of(step % 2 * 8, 8)
@@ -77,37 +94,30 @@
     fields = tuple(enumerate((flow_ref, second_ref, tangent_ref, adjoint_ref)))
     for step in range(6):
         for i, ref in fields:
-            fetch(i, ref, step).start()
-    low = low_half((8, rows))
-    lane = lax.broadcasted_iota(jnp.int32, (8, rows), 1) // radial
-    keep = lane == lax.broadcasted_iota(jnp.int32, (8, rows), 0) % 4
-    for p in range(radial // 2):
-        one = jnp.broadcast_to(wide_ref[2 * p : 2 * p + 1, :], (8, rows))
-        two = jnp.broadcast_to(wide_ref[2 * p + 1 : 2 * p + 2, :], (8, rows))
-        for half, (first, last) in enumerate(((one, two), (two, one))):
-            pair = split(jnp.where(keep, jnp.where(low, first, last), 0.0))
-            for i in range(2):
-                table_ref[half, i, 8 * p : 8 * p + 8, :] = pair[i]
+            fetch(i, ref, step).start(priority=i % 2)
+        if step == 0:
+            fetch_table.start()
+    fetch_table.wait()
 
     def work(step, _):
         for i, ref in fields:
             fetch(i, ref, step).wait()
         c, start = step // 2, pl.multiple_of(step % 2 * 8, 8)
         y = []
-        for half in range(2):
-            x = jnp.concatenate(
-                [field_ref[i, c, pl.ds(start + 4 * half, 4)].reshape(rows, 128) for i in range(4)],
-                axis=1,
+        for p in range(4):
+            x = []
+            for n in range(2):
+                m = start + 2 * p + n
+                x.extend(split(jnp.concatenate([field_ref[i, c, m] for i in range(4)], axis=1)))
+            out = jnp.dot(
+                table_ref[p], jnp.concatenate(x, axis=0), preferred_element_type=F32
             )
-            y.append(table_dot(parts(table_ref.at[half]), x).reshape(radial // 2, 8, 512))
-        first = low_half(y[0].shape)
-        even = jnp.where(first, y[0], y[1])
-        odd = pltpu.roll(jnp.where(first, y[1], y[0]), 4, 1)
-        for parity, z in enumerate((even, odd)):
-            for core in range(2):
-                for which in range(2):
-                    lane = 128 * (2 * core + which)
-                    out_ref[:, parity, core, which, c, pl.ds(start, 8), :] = z[:, :, lane : lane + 128]
+            y.append((out[:128] + out[128:]).reshape(16, 8, 512))
+        for q in range(4):
+            z = pick(y, q, 1)
+            z = pltpu.roll(z, 2 * q, 1) if q else z
+            for i in range(4):
+                out_ref[:, q, i, c, pl.ds(start, 8), :] = z[:, :, 128 * i : 128 * i + 128]
         return _
 
     lax.fori_loop(0, 6, work, 0)
@@ -156,7 +166,7 @@
 def first_kernel(recv_ref, azimuth_ref, zero_ref, two_ref, odd_ref, out_ref, sum_ref):
     def step(c, _):
         axial = (parts(zero_ref), parts(two_ref), parts(odd_ref))
-        azimuth = (parts(azimuth_ref.at[0]), parts(azimuth_ref.at[1]))
+        azimuth = (azimuth_ref[0], azimuth_ref[1])
         y = forward(plane(recv_ref, c), azimuth, axial)
         out_ref[c] = y
         add_to(sum_ref, c, y)
@@ -181,7 +191,7 @@
 ):
     def step(c, _):
         axial = (parts(zero_ref), parts(two_ref), parts(odd_ref))
-        azimuth = (parts(azimuth_ref.at[0]), parts(azimuth_ref.at[1]))
+        azimuth = (azimuth_ref[0], azimuth_ref[1])
         y = forward(plane(recv_ref, 3 + c), azimuth, axial)
         field_ref[c] = y
         add_to(sum_ref, c, y)
@@ -194,10 +204,8 @@
         rhs = own_ref[c] * sum_ref[...] + field_ref[c] * own_sum_ref[...]
         side = []
         for parity in range(2):
-            table = tuple(
-                jnp.concatenate((back_ref[core, parity, i], back_ref[1 - core, parity, i]), axis=0)
-                for i in range(2)
-            )
+            mine, theirs = back_ref[core, parity], back_ref[1 - core, parity]
+            table = jnp.concatenate((mine[:64], theirs[:64], mine[64:], theirs[64:]), axis=0)
             side.append(table_dot(table, rhs[128 * parity : 128 * parity + 128]))
         upper, lower = side[0] + side[1], side[0] - side[1]
         keep_ref[c] = jnp.concatenate((upper[:64], lower[:64]), axis=0)
@@ -224,8 +232,8 @@
 
     def step(c, _):
         rhs = own_ref[c] * sum_ref[...] + other_ref[c] * own_sum_ref[...]
-        e = table_dot(parts(back_ref.at[core, 0]), rhs[:128])
-        o = table_dot(parts(back_ref.at[core, 1]), rhs[128:])
+        e = table_dot(back_ref[core, 0], rhs[:128])
+        o = table_dot(back_ref[core, 1], rhs[128:])
         turned_ref[c] = jnp.concatenate((e + o, e - o), axis=0)
         return _
 
@@ -265,25 +273,24 @@
             result_ref.at[(which, *place)], outs[which].at[place], sems.at[which, c, core]
         )
 
+
     def step(c, _):
-        x = jnp.concatenate(
-            [recv_ref[:, :, core, which, c] for core in range(2) for which in range(2)], axis=3
-        )
-        even, odd = x[:, 0], pltpu.roll(x[:, 1], 4, 1)
-        first = low_half(even.shape)
-        for half in range(2):
-            z = jnp.where(first, even, odd) if half == 0 else jnp.where(first, odd, even)
-            y = table_dot(parts(table_ref.at[half]), z.reshape(4 * radial, 512))
-            for core in range(2):
-                for which in range(2):
-                    lane = 128 * (2 * core + which)
-                    for i in range(4):
-                        m = 8 * core + 4 * half + i
-                        term = y[radial * i : radial * i + radial, lane : lane + 128]
-                        result_ref[which, c, m] = (fields[which][c, m] + time_step * term) * scale_ref[m]
-        for which in range(2):
-            for core in range(2):
-                give(which, c, core).start()
+        for core in range(2):
+            x = []
+            for q in range(4):
+                rows = [recv_ref[:, q, 2 * core + i, c] for i in range(2)]
+                rows = jnp.concatenate(rows, axis=2)
+                x.append(pltpu.roll(rows, 8 - 2 * q, 1) if q else rows)
+            for p in range(4):
+                y = table_dot(table_ref[p], pick(x, p, -1).reshape(128, 256))
+                for n in range(2):
+                    m = 8 * core + 2 * p + n
+                    for which in range(2):
+                        term = y[radial * n : radial * n + radial, 128 * which : 128 * which + 128]
+                        value = (fields[which][c, m] + time_step * term) * scale_ref[m]
+                        result_ref[which, c, m] = value
+            for which in range(2):
+                give(which, c, core).start(priority=which)
         return _
 
     lax.fori_loop(0, 3, step, 0)
@@ -313,25 +320,30 @@
     )(*args)
 
 
-def gather_table(radial):
-    column = np.arange(256)
-    swapped = 2 * (column // 8) + 1 - column % 8 // 4
-    sides = []
-    for j in (column // 4, swapped):
-        keep = np.arange(4)[:, None, None] == (column % 4)[None, None, :]
-        sides.append(halves(np.where(keep, radial.T[:, j][None], 0.0).reshape(256, 256)))
-    return np.stack(sides)
+def radial_tables(radial):
+    t, b, n = np.meshgrid(np.arange(16), np.arange(4), np.arange(2), indexing="ij")
+    there, back = [], []
+    for p in range(4):
+        j = (4 * t + (p - b) % 4).ravel()
+        same = n.ravel()[:, None, None] == np.arange(2)[None, :, None]
+        plain = np.where(same, radial[j][:, None, :], 0.0)
+        high, low = halves(plain)
+        none = np.zeros_like(low)
+        rows = [np.stack(pair, axis=2).reshape(128, 256) for pair in ((high, high), (low, none))]
+        there.append(np.concatenate(rows, axis=0))
+        back.append(stacked(plain.reshape(128, 128).T))
+    return np.stack(there), np.stack(back)
 
 
 def body(saved_flow, saved_adjoint, tangent, second_adjoint, radial_rate):
     radial = radial_table(64)
-    wide = np.tile(radial, (1, 4)).astype(np.float32)
+    there, home_again = radial_tables(radial)
     half, quarter = np.arange(128), np.arange(256)
-    azimuth = np.stack([halves(hartley_table(2 * half + p, half, 256)) for p in range(2)])
+    azimuth = np.stack([stacked(hartley_table(2 * half + p, half, 256)) for p in range(2)])
     kept = [np.array([16 * a + 8 * s + i for a in range(8) for i in range(8)]) for s in range(2)]
     back = np.stack(
         [
-            np.stack([halves(hartley_table(rows, 2 * half + p, 256)) for p in range(2)])
+            np.stack([stacked(hartley_table(rows, 2 * half + p, 256)) for p in range(2)])
             for rows in kept
         ]
     )
@@ -352,18 +364,19 @@
 
     (spread,) = call(
         spread_kernel,
-        [(32, 2, 2, 2, 3, 16, 128)],
+        [(16, 4, 4, 3, 16, 128)],
         *(
             pltpu.with_memory_space_constraint(x, pltpu.HBM)
             for x in (saved_flow, tangent, second_adjoint, saved_adjoint)
         ),
-        wide,
+        pltpu.with_memory_space_constraint(jnp.asarray(there), pltpu.HBM),
         scratch=(
-            pltpu.VMEM((2, 2, 256, 256), BF16),
+            pltpu.VMEM((4, 256, 256), BF16),
             pltpu.VMEM((4, 3, 16, 64, 128), F32),
+            pltpu.SemaphoreType.DMA,
             pltpu.SemaphoreType.DMA((4, 6)),
         ),
-        specs=[LEFT] * 4 + [WHOLE],
+        specs=[LEFT] * 5,
     )
     recv = whole(spread.reshape(128, 6, 16, 128)).reshape(8, 16, 6, 16, 128)
     own, own_sum = call(first_kernel, [(3, *grid), grid], recv, azimuth, *axial)
@@ -391,7 +404,7 @@
         scratch=(pltpu.VMEM(grid, F32), pltpu.VMEM((3, *rows), F32)),
     )
     (send,) = call(join_kernel, [(8, 16, 6, 8, 128)], turned, keep, joined, *axial)
-    home = whole(send.reshape(128, 6, 8, 128)).reshape(32, 2, 2, 2, 3, 8, 128)
+    home = whole(send.reshape(128, 6, 8, 128)).reshape(16, 4, 4, 3, 8, 128)
     shape = tangent.shape
     return tuple(
         call(
@@ -401,7 +414,7 @@
             tangent,
             second_adjoint,
             rate,
-            gather_table(radial),
+            home_again,
             scratch=(
                 pltpu.VMEM((2, *shape), F32),
                 pltpu.VMEM(shape[1:], F32),

time: 157 us -> 156 us (level)
  no operation moved by 1% of the time
where the time goes in v5:
time: 156 us
  blocking collectives  132 us (85%)
  Pallas kernels  20.8 us (13%)
    all_to_all x2, blocking collectives, whole(): return lax.all_to_all(x, ('ax', 'az'), 0, 0, tiled=True)  132 us
    pallas_call x6, Pallas kernels, call(): pl.pallas_call(kernel, out_shape=out, in_specs=specs or [WHOLE] * len(arg...  20.8 us
  transfers between devices with their start and end apart: 2, of which 1 were waited for; matrix products, arithmetic and copies ran while one was open for 0% of the time, Pallas kernels for 5%

profile of v5, /device:TPU:1, one launch (start us, length us, event | category | flops | bytes accessed | tf_op | source)
XLA Modules:
  0.0 155.8 jit_solution(17523180786696851786)
XLA Ops:
  0.6 5.5 %shard_map.131 = f32[16,4,4,3,16,128]{5,4,3,2,1,0:T(8,128)S(1)} custom-call(f32[3,16,64,128]{3,2,1,0:T(8,128)} %flow_ref.1, f32[3,16,64,128]{3,2,1,0:T(8,128)} %tangent_ref.3, f32[3,16,64,128]{3,2,1,0:T(8,128)} %second_ref.3, f32[3,16,64,128]{3,2,1,0:T(8,128)} %adjoint_ref.1, bf16[4,256,256]{2,1,0:T(8,128)(2,1)} %constant.14.clone.radial_ref), custom_call_target="tpu_custom_call" | custom-call | tf_op jit(solution)/shard_map/pallas_call | solution.py:313
  6.1 0.0 copy-start
  6.1 0.0 copy-start.3
  6.1 0.0 copy-start.4
  6.2 0.0 copy-start.5
  6.2 86.4 %all_to_all.10 = f32[128,6,16,128]{3,2,1,0:T(8,128)S(1)} all-to-all(f32[128,6,16,128]{3,2,1,0:T(8,128)S(1)} %bitcast.6), channel_id=1, replica_groups=mesh['ax'=8,'az'=16] {'ax','az'}, dimensions={0} | all-to-all | bytes 12582912 | tf_op jit(solution)/shard_map/all_to_all | solution.py:363
  92.6 0.0 copy-done
  92.6 0.0 copy-start.6
  92.6 3.6 %shard_map.132 = (f32[3,256,1024]{2,1,0:T(8,128)S(1)}, f32[256,1024]{1,0:T(8,128)S(1)}) custom-call(f32[8,16,6,16,128]{4,3,2,1,0:T(8,128)S(1)} %bitcast.4, bf16[2,256,256]{2,1,0:T(8,128)(2,1)S(1)} %copy-done.5, bf16[2,256,256]{2,1,0:T(8,128)(2,1)S(1)} %copy-done.4, bf16[2,256,256]{2,1,0:T(8,128)(2,1)S(1)} %copy-done.3, bf16[2,512,512]{2,1,0:T(8,128)(2,1)S(1)} %copy-done), custom_call_target="tpu_custom_call" | custom-call | tf_op jit(solution)/shard_map/pallas_call | solution.py:313
  96.2 1.3 collective-permute-start
  97.5 5.1 %shard_map.134 = (f32[3,128,1024]{2,1,0:T(8,128)S(1)}, f32[3,128,1024]{2,1,0:T(8,128)S(1)}) custom-call(f32[8,16,6,16,128]{4,3,2,1,0:T(8,128)S(1)} %bitcast.5, f32[3,256,1024]{2,1,0:T(8,128)S(1)} %get-tuple-element.6.own_ref, f32[256,1024]{1,0:T(8,128)S(1)} %get-tuple-element.7.own_sum_ref, bf16[2,256,256]{2,1,0:T(8,128)(2,1)S(1)} %copy-done.5, ...), custom_call_target="tpu_custom_call" | custom-call | tf_op jit(solution)/shard_map/pallas_call | solution.py:313
  102.7 0.1 collective-permute-start.1
  102.8 0.0 collective-permute-done.other_ref
  102.8 2.7 %shard_map.133.tangent_ref = f32[8,16,3,8,128]{4,3,2,1,0:T(8,128)S(1)} custom-call(f32[3,256,1024]{2,1,0:T(8,128)S(1)} %get-tuple-element.6.own_ref, f32[256,1024]{1,0:T(8,128)S(1)} %get-tuple-element.7.own_sum_ref, f32[3,256,1024]{2,1,0:T(8,128)S(1)} %collective-permute-done.other_ref, bf16[2,2,128,256]{3,2,1,0:T(8,128)(2,1)S(1)} %copy-done.6, ...), custom_call_target="tpu_custom_call" | custom-call | tf_op jit(solution)/shard_map/pallas_call | solution.py:313
  105.5 0.7 collective-permute-done.1.other_ref
  106.2 1.2 shard_map.135
  107.4 0.0 copy-start.8
  107.4 0.0 copy-start.1
  107.4 0.0 copy-start.2
  107.4 0.0 copy-start.7
  107.4 45.5 %all_to_all.11 = f32[128,6,8,128]{3,2,1,0:T(8,128)S(1)} all-to-all(f32[128,6,8,128]{3,2,1,0:T(8,128)S(1)} %bitcast.7), channel_id=1, replica_groups=mesh['ax'=8,'az'=16] {'ax','az'}, dimensions={0} | all-to-all | bytes 6291456 | tf_op jit(solution)/shard_map/all_to_all | solution.py:363
  152.9 0.1 broadcast_in_dim.2.rate_ref
  153.0 0.0 copy-done.1
  153.0 2.8 %shard_map.136 = (f32[3,16,64,128]{3,2,1,0:T(8,128)}, f32[3,16,64,128]{3,2,1,0:T(8,128)}) custom-call(f32[16,4,4,3,8,128]{5,4,3,2,1,0:T(8,128)S(1)} %bitcast.8, f32[3,16,64,128]{3,2,1,0:T(8,128)S(1)} %copy-done.1, f32[3,16,64,128]{3,2,1,0:T(8,128)S(1)} %copy-done.2, f32[64,128]{1,0:T(8,128)S(1)} %broadcast_in_dim.2.rate_ref, bf16[4,256,256]{2,1,0:T(8,128)(2,1)S(1)} %copy-done.7), custom_call_target="tpu_custom_call" | custom-call | tf_op jit(solution)/shard_map/pallas_call | solution.py:313
  (7 shorter events, 0.0 us)
Async XLA Ops:
  6.1 86.5 %copy-start = (bf16[2,512,512]{2,1,0:T(8,128)(2,1)S(1)}, bf16[2,512,512]{2,1,0:T(8,128)(2,1)}, u32[]{:S(2)}) copy-start(bf16[2,512,512]{2,1,0:T(8,128)(2,1)} %constant.18.clone.odd_ref) | copy-start | bytes 3145732
  6.1 86.4 %copy-start.3 = (bf16[2,256,256]{2,1,0:T(8,128)(2,1)S(1)}, bf16[2,256,256]{2,1,0:T(8,128)(2,1)}, u32[]{:S(2)}) copy-start(bf16[2,256,256]{2,1,0:T(8,128)(2,1)} %constant.17.clone.two_ref) | copy-start | bytes 786436
  6.1 86.4 %copy-start.4 = (bf16[2,256,256]{2,1,0:T(8,128)(2,1)S(1)}, bf16[2,256,256]{2,1,0:T(8,128)(2,1)}, u32[]{:S(2)}) copy-start(bf16[2,256,256]{2,1,0:T(8,128)(2,1)} %constant.16.clone.zero_ref) | copy-start | bytes 786436
  6.2 86.4 %copy-start.5 = (bf16[2,256,256]{2,1,0:T(8,128)(2,1)S(1)}, bf16[2,256,256]{2,1,0:T(8,128)(2,1)}, u32[]{:S(2)}) copy-start(bf16[2,256,256]{2,1,0:T(8,128)(2,1)} %constant.15.clone.azimuth_ref) | copy-start | bytes 786436
  92.6 4.9 %copy-start.6 = (bf16[2,2,128,256]{3,2,1,0:T(8,128)(2,1)S(1)}, bf16[2,2,128,256]{3,2,1,0:T(8,128)(2,1)}, u32[]{:S(2)}) copy-start(bf16[2,2,128,256]{3,2,1,0:T(8,128)(2,1)} %constant.19.clone.back_ref) | copy-start | bytes 786436
  96.2 6.6 %collective-permute-start = (f32[3,256,1024]{2,1,0:T(8,128)S(1)}, f32[3,256,1024]{2,1,0:T(8,128)S(1)}, u32[]{:S(2)}, u32[]{:S(2)}) collective-permute-start(f32[3,256,1024]{2,1,0:T(8,128)S(1)} %get-tuple-element.6.own_ref), channel_id=1, source_target_pairs={{0,1},{1,0},{2,3},{3,2},{4,5},{5,4},{6,7},{7,6},{8,9},{9,8},{10,11... | collective-permute-start | bytes 9437192 | tf_op jit(solution)/shard_map/ppermute | solution.py:360
  102.7 3.5 %collective-permute-start.1 = (f32[3,128,1024]{2,1,0:T(8,128)S(1)}, f32[3,128,1024]{2,1,0:T(8,128)S(1)}, u32[]{:S(2)}, u32[]{:S(2)}) collective-permute-start(f32[3,128,1024]{2,1,0:T(8,128)S(1)} %get-tuple-element.9), channel_id=1, source_target_pairs={{0,1},{1,0},{2,3},{3,2},{4,5},{5,4},{6,7},{7,6},{8,9},{9,8},{10,11... | collective-permute-start | bytes 4718600 | tf_op jit(solution)/shard_map/ppermute | solution.py:360
  107.4 45.5 %copy-start.8 = (f32[64]{0:T(128)S(1)}, f32[64]{0:T(128)}, u32[]{:S(2)}) copy-start(f32[64]{0:T(128)} %param.16) | copy-start | bytes 772
  107.4 45.6 %copy-start.1 = (f32[3,16,64,128]{3,2,1,0:T(8,128)S(1)}, f32[3,16,64,128]{3,2,1,0:T(8,128)}, u32[]{:S(2)}) copy-start(f32[3,16,64,128]{3,2,1,0:T(8,128)} %tangent_ref.3) | copy-start | bytes 4718596
  107.4 45.6 %copy-start.2 = (f32[3,16,64,128]{3,2,1,0:T(8,128)S(1)}, f32[3,16,64,128]{3,2,1,0:T(8,128)}, u32[]{:S(2)}) copy-start(f32[3,16,64,128]{3,2,1,0:T(8,128)} %second_ref.3) | copy-start | bytes 4718596
  107.4 45.6 %copy-start.7 = (bf16[4,256,256]{2,1,0:T(8,128)(2,1)S(1)}, bf16[4,256,256]{2,1,0:T(8,128)(2,1)}, u32[]{:S(2)}) copy-start(bf16[4,256,256]{2,1,0:T(8,128)(2,1)} %constant.20.clone.table_ref) | copy-start | bytes 1572868

commit v6 on v5

--- a/solution.py
+++ b/solution.py
@@ -43,6 +43,11 @@
 def stacked(table):
     high, low = halves(table)
     return np.block([[high, high], [low, np.zeros_like(low)]])
+
+
+def lay(high, low):
+    right = jnp.concatenate((high, jnp.zeros_like(low)), axis=0)
+    return jnp.concatenate((jnp.concatenate((high, low), axis=0), right), axis=1)
 
 
 def table_dot(table, x):
@@ -99,28 +104,28 @@
             fetch_table.start()
     fetch_table.wait()
 
-    def work(step, _):
-        for i, ref in fields:
-            fetch(i, ref, step).wait()
-        c, start = step // 2, pl.multiple_of(step % 2 * 8, 8)
-        y = []
-        for p in range(4):
-            x = []
-            for n in range(2):
-                m = start + 2 * p + n
-                x.extend(split(jnp.concatenate([field_ref[i, c, m] for i in range(4)], axis=1)))
-            out = jnp.dot(
-                table_ref[p], jnp.concatenate(x, axis=0), preferred_element_type=F32
-            )
-            y.append((out[:128] + out[128:]).reshape(16, 8, 512))
-        for q in range(4):
-            z = pick(y, q, 1)
-            z = pltpu.roll(z, 2 * q, 1) if q else z
-            for i in range(4):
-                out_ref[:, q, i, c, pl.ds(start, 8), :] = z[:, :, 128 * i : 128 * i + 128]
-        return _
-
-    lax.fori_loop(0, 6, work, 0)
+    def work(c, _):
+        for step in (2 * c, 2 * c + 1):
+            for i, ref in fields:
+                fetch(i, ref, step).wait()
+        for start in (0, 8):
+            y = []
+            for p in range(4):
+                x = []
+                for m in (start + 2 * p, start + 2 * p + 1):
+                    x.extend(split(jnp.concatenate([field_ref[i, c, m] for i in range(4)], axis=1)))
+                out = jnp.dot(
+                    table_ref[p], jnp.concatenate(x, axis=0), preferred_element_type=F32
+                )
+                y.append((out[:128] + out[128:]).reshape(16, 8, 512))
+            for q in range(4):
+                z = pick(y, q, 1)
+                z = pltpu.roll(z, 2 * q, 1) if q else z
+                for i in range(4):
+                    out_ref[:, q, i, c, start : start + 8, :] = z[:, :, 128 * i : 128 * i + 128]
+        return _
+
+    lax.fori_loop(0, 3, work, 0)
 
 
 def forward(x, azimuth, axial):
@@ -166,7 +171,7 @@
 def first_kernel(recv_ref, azimuth_ref, zero_ref, two_ref, odd_ref, out_ref, sum_ref):
     def step(c, _):
         axial = (parts(zero_ref), parts(two_ref), parts(odd_ref))
-        azimuth = (azimuth_ref[0], azimuth_ref[1])
+        azimuth = tuple(lay(*parts(azimuth_ref.at[p])) for p in range(2))
         y = forward(plane(recv_ref, c), azimuth, axial)
         out_ref[c] = y
         add_to(sum_ref, c, y)
@@ -191,7 +196,7 @@
 ):
     def step(c, _):
         axial = (parts(zero_ref), parts(two_ref), parts(odd_ref))
-        azimuth = (azimuth_ref[0], azimuth_ref[1])
+        azimuth = tuple(lay(*parts(azimuth_ref.at[p])) for p in range(2))
         y = forward(plane(recv_ref, 3 + c), azimuth, axial)
         field_ref[c] = y
         add_to(sum_ref, c, y)
@@ -204,8 +209,8 @@
         rhs = own_ref[c] * sum_ref[...] + field_ref[c] * own_sum_ref[...]
         side = []
         for parity in range(2):
-            mine, theirs = back_ref[core, parity], back_ref[1 - core, parity]
-            table = jnp.concatenate((mine[:64], theirs[:64], mine[64:], theirs[64:]), axis=0)
+            mine, theirs = back_ref.at[core, parity], back_ref.at[1 - core, parity]
+            table = lay(*(jnp.concatenate((mine[i], theirs[i]), axis=0) for i in range(2)))
             side.append(table_dot(table, rhs[128 * parity : 128 * parity + 128]))
         upper, lower = side[0] + side[1], side[0] - side[1]
         keep_ref[c] = jnp.concatenate((upper[:64], lower[:64]), axis=0)
@@ -232,8 +237,8 @@
 
     def step(c, _):
         rhs = own_ref[c] * sum_ref[...] + other_ref[c] * own_sum_ref[...]
-        e = table_dot(back_ref[core, 0], rhs[:128])
-        o = table_dot(back_ref[core, 1], rhs[128:])
+        e = table_dot(lay(*parts(back_ref.at[core, 0])), rhs[:128])
+        o = table_dot(lay(*parts(back_ref.at[core, 1])), rhs[128:])
         turned_ref[c] = jnp.concatenate((e + o, e - o), axis=0)
         return _
 
@@ -339,11 +344,11 @@
     radial = radial_table(64)
     there, home_again = radial_tables(radial)
     half, quarter = np.arange(128), np.arange(256)
-    azimuth = np.stack([stacked(hartley_table(2 * half + p, half, 256)) for p in range(2)])
+    azimuth = np.stack([halves(hartley_table(2 * half + p, half, 256)) for p in range(2)])
     kept = [np.array([16 * a + 8 * s + i for a in range(8) for i in range(8)]) for s in range(2)]
     back = np.stack(
         [
-            np.stack([stacked(hartley_table(rows, 2 * half + p, 256)) for p in range(2)])
+            np.stack([halves(hartley_table(rows, 2 * half + p, 256)) for p in range(2)])
             for rows in kept
         ]
     )

time: 156 us -> 156 us (level)
  no operation moved by 1% of the time
where the time goes in v6:
time: 156 us
  blocking collectives  132 us (85%)
  Pallas kernels  20.6 us (13%)
    all_to_all x2, blocking collectives, whole(): return lax.all_to_all(x, ('ax', 'az'), 0, 0, tiled=True)  132 us
    pallas_call x6, Pallas kernels, call(): pl.pallas_call(kernel, out_shape=out, in_specs=specs or [WHOLE] * len(arg...  20.6 us
  transfers between devices with their start and end apart: 2, of which 1 were waited for; matrix products, arithmetic and copies ran while one was open for 0% of the time, Pallas kernels for 5%

profile of v6, /device:TPU:1, one launch (start us, length us, event | category | flops | bytes accessed | tf_op | source)
XLA Modules:
  0.0 155.6 jit_solution(7486815076811104478)
XLA Ops:
  0.6 5.2 %shard_map.131 = f32[16,4,4,3,16,128]{5,4,3,2,1,0:T(8,128)S(1)} custom-call(f32[3,16,64,128]{3,2,1,0:T(8,128)} %flow_ref.1, f32[3,16,64,128]{3,2,1,0:T(8,128)} %tangent_ref.3, f32[3,16,64,128]{3,2,1,0:T(8,128)} %second_ref.3, f32[3,16,64,128]{3,2,1,0:T(8,128)} %adjoint_ref.1, bf16[4,256,256]{2,1,0:T(8,128)(2,1)} %constant.14.clone.radial_ref), custom_call_target="tpu_custom_call" | custom-call | tf_op jit(solution)/shard_map/pallas_call | solution.py:318
  5.9 0.0 copy-start
  5.9 0.0 copy-start.3
  5.9 0.0 copy-start.4
  5.9 0.0 copy-start.5
  5.9 86.4 %all_to_all.10 = f32[128,6,16,128]{3,2,1,0:T(8,128)S(1)} all-to-all(f32[128,6,16,128]{3,2,1,0:T(8,128)S(1)} %bitcast.6), channel_id=1, replica_groups=mesh['ax'=8,'az'=16] {'ax','az'}, dimensions={0} | all-to-all | bytes 12582912 | tf_op jit(solution)/shard_map/all_to_all | solution.py:368
  92.3 0.0 copy-done
  92.3 0.0 copy-done.3
  92.3 0.0 copy-start.6
  92.4 3.7 %shard_map.132 = (f32[3,256,1024]{2,1,0:T(8,128)S(1)}, f32[256,1024]{1,0:T(8,128)S(1)}) custom-call(f32[8,16,6,16,128]{4,3,2,1,0:T(8,128)S(1)} %bitcast.4, bf16[2,2,128,128]{3,2,1,0:T(8,128)(2,1)S(1)} %copy-done.5, bf16[2,256,256]{2,1,0:T(8,128)(2,1)S(1)} %copy-done.4, bf16[2,256,256]{2,1,0:T(8,128)(2,1)S(1)} %copy-done.3, bf16[2,512,512]{2,1,0:T(8,128)(2,1)S(1)} %copy-done), custom_call_target="tpu_custom_call" | custom-call | tf_op jit(solution)/shard_map/pallas_call | solution.py:318
  96.0 1.3 collective-permute-start
  97.4 5.1 %shard_map.134 = (f32[3,128,1024]{2,1,0:T(8,128)S(1)}, f32[3,128,1024]{2,1,0:T(8,128)S(1)}) custom-call(f32[8,16,6,16,128]{4,3,2,1,0:T(8,128)S(1)} %bitcast.5, f32[3,256,1024]{2,1,0:T(8,128)S(1)} %get-tuple-element.6.own_ref, f32[256,1024]{1,0:T(8,128)S(1)} %get-tuple-element.7.own_sum_ref, bf16[2,2,128,128]{3,2,1,0:T(8,128)(2,1)S(1)} %copy-done.5, ...), custom_call_target="tpu_custom_call" | custom-call | tf_op jit(solution)/shard_map/pallas_call | solution.py:318
  102.5 0.1 collective-permute-start.1
  102.6 0.0 collective-permute-done.other_ref
  102.7 2.6 %shard_map.133.tangent_ref = f32[8,16,3,8,128]{4,3,2,1,0:T(8,128)S(1)} custom-call(f32[3,256,1024]{2,1,0:T(8,128)S(1)} %get-tuple-element.6.own_ref, f32[256,1024]{1,0:T(8,128)S(1)} %get-tuple-element.7.own_sum_ref, f32[3,256,1024]{2,1,0:T(8,128)S(1)} %collective-permute-done.other_ref, bf16[2,2,2,64,128]{4,3,2,1,0:T(8,128)(2,1)S(1)} %copy-done.6, ...), custom_call_target="tpu_custom_call" | custom-call | tf_op jit(solution)/shard_map/pallas_call | solution.py:318
  105.3 0.7 collective-permute-done.1.other_ref
  106.0 1.2 shard_map.135
  107.2 0.0 copy-start.8
  107.2 0.0 copy-start.1
  107.2 0.0 copy-start.2
  107.2 0.0 copy-start.7
  107.3 45.4 %all_to_all.11 = f32[128,6,8,128]{3,2,1,0:T(8,128)S(1)} all-to-all(f32[128,6,8,128]{3,2,1,0:T(8,128)S(1)} %bitcast.7), channel_id=1, replica_groups=mesh['ax'=8,'az'=16] {'ax','az'}, dimensions={0} | all-to-all | bytes 6291456 | tf_op jit(solution)/shard_map/all_to_all | solution.py:368
  152.7 0.1 broadcast_in_dim.2.rate_ref
  152.8 2.8 %shard_map.136 = (f32[3,16,64,128]{3,2,1,0:T(8,128)}, f32[3,16,64,128]{3,2,1,0:T(8,128)}) custom-call(f32[16,4,4,3,8,128]{5,4,3,2,1,0:T(8,128)S(1)} %bitcast.8, f32[3,16,64,128]{3,2,1,0:T(8,128)S(1)} %copy-done.1, f32[3,16,64,128]{3,2,1,0:T(8,128)S(1)} %copy-done.2, f32[64,128]{1,0:T(8,128)S(1)} %broadcast_in_dim.2.rate_ref, bf16[4,256,256]{2,1,0:T(8,128)(2,1)S(1)} %copy-done.7), custom_call_target="tpu_custom_call" | custom-call | tf_op jit(solution)/shard_map/pallas_call | solution.py:318
  (7 shorter events, 0.0 us)
Async XLA Ops:
  5.9 86.5 %copy-start = (bf16[2,512,512]{2,1,0:T(8,128)(2,1)S(1)}, bf16[2,512,512]{2,1,0:T(8,128)(2,1)}, u32[]{:S(2)}) copy-start(bf16[2,512,512]{2,1,0:T(8,128)(2,1)} %constant.18.clone.odd_ref) | copy-start | bytes 3145732
  5.9 86.4 %copy-start.3 = (bf16[2,256,256]{2,1,0:T(8,128)(2,1)S(1)}, bf16[2,256,256]{2,1,0:T(8,128)(2,1)}, u32[]{:S(2)}) copy-start(bf16[2,256,256]{2,1,0:T(8,128)(2,1)} %constant.17.clone.two_ref) | copy-start | bytes 786436
  5.9 86.4 %copy-start.4 = (bf16[2,256,256]{2,1,0:T(8,128)(2,1)S(1)}, bf16[2,256,256]{2,1,0:T(8,128)(2,1)}, u32[]{:S(2)}) copy-start(bf16[2,256,256]{2,1,0:T(8,128)(2,1)} %constant.16.clone.zero_ref) | copy-start | bytes 786436
  5.9 86.4 %copy-start.5 = (bf16[2,2,128,128]{3,2,1,0:T(8,128)(2,1)S(1)}, bf16[2,2,128,128]{3,2,1,0:T(8,128)(2,1)}, u32[]{:S(2)}) copy-start(bf16[2,2,128,128]{3,2,1,0:T(8,128)(2,1)} %constant.15.clone.azimuth_ref) | copy-start | bytes 393220
  92.3 5.0 %copy-start.6 = (bf16[2,2,2,64,128]{4,3,2,1,0:T(8,128)(2,1)S(1)}, bf16[2,2,2,64,128]{4,3,2,1,0:T(8,128)(2,1)}, u32[]{:S(2)}) copy-start(bf16[2,2,2,64,128]{4,3,2,1,0:T(8,128)(2,1)} %constant.19.clone.back_ref) | copy-start | bytes 393220
  96.0 6.6 %collective-permute-start = (f32[3,256,1024]{2,1,0:T(8,128)S(1)}, f32[3,256,1024]{2,1,0:T(8,128)S(1)}, u32[]{:S(2)}, u32[]{:S(2)}) collective-permute-start(f32[3,256,1024]{2,1,0:T(8,128)S(1)} %get-tuple-element.6.own_ref), channel_id=1, source_target_pairs={{0,1},{1,0},{2,3},{3,2},{4,5},{5,4},{6,7},{7,6},{8,9},{9,8},{10,11... | collective-permute-start | bytes 9437192 | tf_op jit(solution)/shard_map/ppermute | solution.py:365
  102.5 3.5 %collective-permute-start.1 = (f32[3,128,1024]{2,1,0:T(8,128)S(1)}, f32[3,128,1024]{2,1,0:T(8,128)S(1)}, u32[]{:S(2)}, u32[]{:S(2)}) collective-permute-start(f32[3,128,1024]{2,1,0:T(8,128)S(1)} %get-tuple-element.9), channel_id=1, source_target_pairs={{0,1},{1,0},{2,3},{3,2},{4,5},{5,4},{6,7},{7,6},{8,9},{9,8},{10,11... | collective-permute-start | bytes 4718600 | tf_op jit(solution)/shard_map/ppermute | solution.py:365
  107.2 45.5 %copy-start.8 = (f32[64]{0:T(128)S(1)}, f32[64]{0:T(128)}, u32[]{:S(2)}) copy-start(f32[64]{0:T(128)} %param.16) | copy-start | bytes 772
  107.2 45.5 %copy-start.1 = (f32[3,16,64,128]{3,2,1,0:T(8,128)S(1)}, f32[3,16,64,128]{3,2,1,0:T(8,128)}, u32[]{:S(2)}) copy-start(f32[3,16,64,128]{3,2,1,0:T(8,128)} %tangent_ref.3) | copy-start | bytes 4718596
  107.2 45.5 %copy-start.2 = (f32[3,16,64,128]{3,2,1,0:T(8,128)S(1)}, f32[3,16,64,128]{3,2,1,0:T(8,128)}, u32[]{:S(2)}) copy-start(f32[3,16,64,128]{3,2,1,0:T(8,128)} %second_ref.3) | copy-start | bytes 4718596
  107.2 45.5 %copy-start.7 = (bf16[4,256,256]{2,1,0:T(8,128)(2,1)S(1)}, bf16[4,256,256]{2,1,0:T(8,128)(2,1)}, u32[]{:S(2)}) copy-start(bf16[4,256,256]{2,1,0:T(8,128)(2,1)} %constant.20.clone.table_ref) | copy-start | bytes 1572868

commit v7 on v6

--- a/solution.py
+++ b/solution.py
@@ -58,11 +58,12 @@
 
 def dot_table(x, table, turned):
     high, low = split(x)
-    left = jnp.concatenate((high, low, high), axis=1)
-    right = jnp.concatenate((table[0], table[0], table[1]), axis=1 if turned else 0)
-    return lax.dot_general(
-        left, right, (((1,), (1 if turned else 0,)), ((), ())), preferred_element_type=F32
-    )
+    numbers = (((1,), (1 if turned else 0,)), ((), ()))
+    both = lax.dot_general(
+        jnp.concatenate((high, low), axis=0), table[0], numbers, preferred_element_type=F32
+    )
+    rest = lax.dot_general(high, table[1], numbers, preferred_element_type=F32)
+    return both[: x.shape[0]] + both[x.shape[0] :] + rest
 
 
 def parts(ref):
@@ -91,23 +92,20 @@
 ):
     fetch_table = pltpu.make_async_copy(radial_ref, table_ref, sem)
 
-    def fetch(i, ref, step):
-        c, start = step // 2, pl.multiple_of(step % 2 * 8, 8)
-        place = (c, pl.ds(start, 8))
-        return pltpu.make_async_copy(ref.at[place], field_ref.at[(i, *place)], sems.at[i, step])
+    def fetch(i, ref, c):
+        return pltpu.make_async_copy(ref.at[c], field_ref.at[i, c], sems.at[i, c])
 
     fields = tuple(enumerate((flow_ref, second_ref, tangent_ref, adjoint_ref)))
-    for step in range(6):
+    for c in range(3):
         for i, ref in fields:
-            fetch(i, ref, step).start(priority=i % 2)
-        if step == 0:
+            fetch(i, ref, c).start(priority=i % 2)
+        if c == 0:
             fetch_table.start()
     fetch_table.wait()
 
     def work(c, _):
-        for step in (2 * c, 2 * c + 1):
-            for i, ref in fields:
-                fetch(i, ref, step).wait()
+        for i, ref in fields:
+            fetch(i, ref, c).wait()
         for start in (0, 8):
             y = []
             for p in range(4):
@@ -379,7 +377,7 @@
             pltpu.VMEM((4, 256, 256), BF16),
             pltpu.VMEM((4, 3, 16, 64, 128), F32),
             pltpu.SemaphoreType.DMA,
-            pltpu.SemaphoreType.DMA((4, 6)),
+            pltpu.SemaphoreType.DMA((4, 3)),
         ),
         specs=[LEFT] * 5,
     )

time: 156 us -> 156 us (level)
  transfers between devices with their start and end apart: 2 -> 2, of which waited for: 1 -> 2; matrix products, arithmetic and copies ran while one was open for 0% -> 0% of each run, Pallas kernels for 5% -> 5%
where the time goes in v7:
time: 156 us; the launch traced here: 155 us
  blocking collectives  132 us (85%)
  Pallas kernels  20.4 us (13%)
    all_to_all x2, blocking collectives, whole(): return lax.all_to_all(x, ('ax', 'az'), 0, 0, tiled=True)  132 us
    pallas_call x6, Pallas kernels, call(): pl.pallas_call(kernel, out_shape=out, in_specs=specs or [WHOLE] * len(arg...  20.4 us
  transfers between devices with their start and end apart: 2, of which 2 were waited for; matrix products, arithmetic and copies ran while one was open for 0% of the time, Pallas kernels for 5%

profile of v7, /device:TPU:1, one launch (start us, length us, event | category | flops | bytes accessed | tf_op | source)
XLA Modules:
  0.0 155.4 jit_solution(16187590547595324431)
XLA Ops:
  0.6 5.1 %shard_map.131 = f32[16,4,4,3,16,128]{5,4,3,2,1,0:T(8,128)S(1)} custom-call(f32[3,16,64,128]{3,2,1,0:T(8,128)} %flow_ref.1, f32[3,16,64,128]{3,2,1,0:T(8,128)} %tangent_ref.3, f32[3,16,64,128]{3,2,1,0:T(8,128)} %second_ref.3, f32[3,16,64,128]{3,2,1,0:T(8,128)} %adjoint_ref.1, bf16[4,256,256]{2,1,0:T(8,128)(2,1)} %constant.14.clone.radial_ref), custom_call_target="tpu_custom_call" | custom-call | tf_op jit(solution)/shard_map/pallas_call | solution.py:316
  5.8 0.0 copy-start
  5.8 0.0 copy-start.3
  5.8 0.0 copy-start.4
  5.8 0.0 copy-start.5
  5.8 86.4 %all_to_all.10 = f32[128,6,16,128]{3,2,1,0:T(8,128)S(1)} all-to-all(f32[128,6,16,128]{3,2,1,0:T(8,128)S(1)} %bitcast.6), channel_id=1, replica_groups=mesh['ax'=8,'az'=16] {'ax','az'}, dimensions={0} | all-to-all | bytes 12582912 | tf_op jit(solution)/shard_map/all_to_all | solution.py:366
  92.2 0.0 copy-done
  92.2 0.0 copy-start.6
  92.3 3.6 %shard_map.132 = (f32[3,256,1024]{2,1,0:T(8,128)S(1)}, f32[256,1024]{1,0:T(8,128)S(1)}) custom-call(f32[8,16,6,16,128]{4,3,2,1,0:T(8,128)S(1)} %bitcast.4, bf16[2,2,128,128]{3,2,1,0:T(8,128)(2,1)S(1)} %copy-done.5, bf16[2,256,256]{2,1,0:T(8,128)(2,1)S(1)} %copy-done.4, bf16[2,256,256]{2,1,0:T(8,128)(2,1)S(1)} %copy-done.3, bf16[2,512,512]{2,1,0:T(8,128)(2,1)S(1)} %copy-done), custom_call_target="tpu_custom_call" | custom-call | tf_op jit(solution)/shard_map/pallas_call | solution.py:316
  95.8 1.4 collective-permute-start
  97.2 5.1 %shard_map.134 = (f32[3,128,1024]{2,1,0:T(8,128)S(1)}, f32[3,128,1024]{2,1,0:T(8,128)S(1)}) custom-call(f32[8,16,6,16,128]{4,3,2,1,0:T(8,128)S(1)} %bitcast.5, f32[3,256,1024]{2,1,0:T(8,128)S(1)} %get-tuple-element.6.own_ref, f32[256,1024]{1,0:T(8,128)S(1)} %get-tuple-element.7.own_sum_ref, bf16[2,2,128,128]{3,2,1,0:T(8,128)(2,1)S(1)} %copy-done.5, ...), custom_call_target="tpu_custom_call" | custom-call | tf_op jit(solution)/shard_map/pallas_call | solution.py:316
  102.3 0.1 collective-permute-start.1
  102.4 0.1 collective-permute-done.other_ref
  102.5 2.6 %shard_map.133.tangent_ref = f32[8,16,3,8,128]{4,3,2,1,0:T(8,128)S(1)} custom-call(f32[3,256,1024]{2,1,0:T(8,128)S(1)} %get-tuple-element.6.own_ref, f32[256,1024]{1,0:T(8,128)S(1)} %get-tuple-element.7.own_sum_ref, f32[3,256,1024]{2,1,0:T(8,128)S(1)} %collective-permute-done.other_ref, bf16[2,2,2,64,128]{4,3,2,1,0:T(8,128)(2,1)S(1)} %copy-done.6, ...), custom_call_target="tpu_custom_call" | custom-call | tf_op jit(solution)/shard_map/pallas_call | solution.py:316
  105.1 0.7 collective-permute-done.1.other_ref
  105.8 1.2 shard_map.135
  107.0 0.0 copy-start.8
  107.0 0.0 copy-start.1
  107.1 0.0 copy-start.2
  107.1 0.0 copy-start.7
  107.1 45.5 %all_to_all.11 = f32[128,6,8,128]{3,2,1,0:T(8,128)S(1)} all-to-all(f32[128,6,8,128]{3,2,1,0:T(8,128)S(1)} %bitcast.7), channel_id=1, replica_groups=mesh['ax'=8,'az'=16] {'ax','az'}, dimensions={0} | all-to-all | bytes 6291456 | tf_op jit(solution)/shard_map/all_to_all | solution.py:366
  152.6 0.1 broadcast_in_dim.2.rate_ref
  152.6 0.0 copy-done.1
  152.7 2.8 %shard_map.136 = (f32[3,16,64,128]{3,2,1,0:T(8,128)}, f32[3,16,64,128]{3,2,1,0:T(8,128)}) custom-call(f32[16,4,4,3,8,128]{5,4,3,2,1,0:T(8,128)S(1)} %bitcast.8, f32[3,16,64,128]{3,2,1,0:T(8,128)S(1)} %copy-done.1, f32[3,16,64,128]{3,2,1,0:T(8,128)S(1)} %copy-done.2, f32[64,128]{1,0:T(8,128)S(1)} %broadcast_in_dim.2.rate_ref, bf16[4,256,256]{2,1,0:T(8,128)(2,1)S(1)} %copy-done.7), custom_call_target="tpu_custom_call" | custom-call | tf_op jit(solution)/shard_map/pallas_call | solution.py:316
  (7 shorter events, 0.0 us)
Async XLA Ops:
  5.8 86.5 %copy-start = (bf16[2,512,512]{2,1,0:T(8,128)(2,1)S(1)}, bf16[2,512,512]{2,1,0:T(8,128)(2,1)}, u32[]{:S(2)}) copy-start(bf16[2,512,512]{2,1,0:T(8,128)(2,1)} %constant.18.clone.odd_ref) | copy-start | bytes 3145732
  5.8 86.5 %copy-start.3 = (bf16[2,256,256]{2,1,0:T(8,128)(2,1)S(1)}, bf16[2,256,256]{2,1,0:T(8,128)(2,1)}, u32[]{:S(2)}) copy-start(bf16[2,256,256]{2,1,0:T(8,128)(2,1)} %constant.17.clone.two_ref) | copy-start | bytes 786436
  5.8 86.4 %copy-start.4 = (bf16[2,256,256]{2,1,0:T(8,128)(2,1)S(1)}, bf16[2,256,256]{2,1,0:T(8,128)(2,1)}, u32[]{:S(2)}) copy-start(bf16[2,256,256]{2,1,0:T(8,128)(2,1)} %constant.16.clone.zero_ref) | copy-start | bytes 786436
  5.8 86.4 %copy-start.5 = (bf16[2,2,128,128]{3,2,1,0:T(8,128)(2,1)S(1)}, bf16[2,2,128,128]{3,2,1,0:T(8,128)(2,1)}, u32[]{:S(2)}) copy-start(bf16[2,2,128,128]{3,2,1,0:T(8,128)(2,1)} %constant.15.clone.azimuth_ref) | copy-start | bytes 393220
  92.2 5.0 %copy-start.6 = (bf16[2,2,2,64,128]{4,3,2,1,0:T(8,128)(2,1)S(1)}, bf16[2,2,2,64,128]{4,3,2,1,0:T(8,128)(2,1)}, u32[]{:S(2)}) copy-start(bf16[2,2,2,64,128]{4,3,2,1,0:T(8,128)(2,1)} %constant.19.clone.back_ref) | copy-start | bytes 393220
  95.8 6.6 %collective-permute-start = (f32[3,256,1024]{2,1,0:T(8,128)S(1)}, f32[3,256,1024]{2,1,0:T(8,128)S(1)}, u32[]{:S(2)}, u32[]{:S(2)}) collective-permute-start(f32[3,256,1024]{2,1,0:T(8,128)S(1)} %get-tuple-element.6.own_ref), channel_id=1, source_target_pairs={{0,1},{1,0},{2,3},{3,2},{4,5},{5,4},{6,7},{7,6},{8,9},{9,8},{10,11... | collective-permute-start | bytes 9437192 | tf_op jit(solution)/shard_map/ppermute | solution.py:363
  102.3 3.5 %collective-permute-start.1 = (f32[3,128,1024]{2,1,0:T(8,128)S(1)}, f32[3,128,1024]{2,1,0:T(8,128)S(1)}, u32[]{:S(2)}, u32[]{:S(2)}) collective-permute-start(f32[3,128,1024]{2,1,0:T(8,128)S(1)} %get-tuple-element.9), channel_id=1, source_target_pairs={{0,1},{1,0},{2,3},{3,2},{4,5},{5,4},{6,7},{7,6},{8,9},{9,8},{10,11... | collective-permute-start | bytes 4718600 | tf_op jit(solution)/shard_map/ppermute | solution.py:363
  107.0 45.5 %copy-start.8 = (f32[64]{0:T(128)S(1)}, f32[64]{0:T(128)}, u32[]{:S(2)}) copy-start(f32[64]{0:T(128)} %param.16) | copy-start | bytes 772
  107.0 45.6 %copy-start.1 = (f32[3,16,64,128]{3,2,1,0:T(8,128)S(1)}, f32[3,16,64,128]{3,2,1,0:T(8,128)}, u32[]{:S(2)}) copy-start(f32[3,16,64,128]{3,2,1,0:T(8,128)} %tangent_ref.3) | copy-start | bytes 4718596
  107.1 45.6 %copy-start.2 = (f32[3,16,64,128]{3,2,1,0:T(8,128)S(1)}, f32[3,16,64,128]{3,2,1,0:T(8,128)}, u32[]{:S(2)}) copy-start(f32[3,16,64,128]{3,2,1,0:T(8,128)} %second_ref.3) | copy-start | bytes 4718596
  107.1 45.6 %copy-start.7 = (bf16[4,256,256]{2,1,0:T(8,128)(2,1)S(1)}, bf16[4,256,256]{2,1,0:T(8,128)(2,1)}, u32[]{:S(2)}) copy-start(bf16[4,256,256]{2,1,0:T(8,128)(2,1)} %constant.20.clone.table_ref) | copy-start | bytes 1572868

commit v8 on v7

--- a/solution.py
+++ b/solution.py
@@ -92,21 +92,26 @@
 ):
     fetch_table = pltpu.make_async_copy(radial_ref, table_ref, sem)
 
-    def fetch(i, ref, c):
-        return pltpu.make_async_copy(ref.at[c], field_ref.at[i, c], sems.at[i, c])
+    def fetch(i, ref, c, start):
+        place = (c, pl.ds(start, 8))
+        return pltpu.make_async_copy(
+            ref.at[place], field_ref.at[(i, *place)], sems.at[i, c, start // 8]
+        )
 
     fields = tuple(enumerate((flow_ref, second_ref, tangent_ref, adjoint_ref)))
     for c in range(3):
-        for i, ref in fields:
-            fetch(i, ref, c).start(priority=i % 2)
-        if c == 0:
-            fetch_table.start()
+        for start in (0, 8):
+            for i, ref in fields:
+                fetch(i, ref, c, start).start(priority=i % 2)
+            if c == start == 0:
+                fetch_table.start()
     fetch_table.wait()
 
-    def work(c, _):
-        for i, ref in fields:
-            fetch(i, ref, c).wait()
-        for start in (0, 8):
+    def work(*groups):
+        for place in groups:
+            for i, ref in fields:
+                fetch(i, ref, *place).wait()
+        for c, start in groups:
             y = []
             for p in range(4):
                 x = []
@@ -121,9 +126,14 @@
                 z = pltpu.roll(z, 2 * q, 1) if q else z
                 for i in range(4):
                     out_ref[:, q, i, c, start : start + 8, :] = z[:, :, 128 * i : 128 * i + 128]
-        return _
-
-    lax.fori_loop(0, 3, work, 0)
+
+    def pair(c, _):
+        work((c, 8), (c + 1, 0))
+        return _
+
+    work((0, 0))
+    lax.fori_loop(0, 2, pair, 0)
+    work((2, 8))
 
 
 def forward(x, azimuth, axial):
@@ -377,7 +387,7 @@
             pltpu.VMEM((4, 256, 256), BF16),
             pltpu.VMEM((4, 3, 16, 64, 128), F32),
             pltpu.SemaphoreType.DMA,
-            pltpu.SemaphoreType.DMA((4, 3)),
+            pltpu.SemaphoreType.DMA((4, 3, 2)),
         ),
         specs=[LEFT] * 5,
     )

time: 156 us -> 156 us (level)
  no operation moved by 1% of the time
where the time goes in v8:
time: 156 us
  blocking collectives  132 us (85%)
  Pallas kernels  20.5 us (13%)
    all_to_all x2, blocking collectives, whole(): return lax.all_to_all(x, ('ax', 'az'), 0, 0, tiled=True)  132 us
    pallas_call x6, Pallas kernels, call(): pl.pallas_call(kernel, out_shape=out, in_specs=specs or [WHOLE] * len(arg...  20.5 us
  transfers between devices with their start and end apart: 2, of which 2 were waited for; matrix products, arithmetic and copies ran while one was open for 0% of the time, Pallas kernels for 5%

profile of v8, /device:TPU:1, one launch (start us, length us, event | category | flops | bytes accessed | tf_op | source)
XLA Modules:
  0.0 155.5 jit_solution(16019519619304667306)
XLA Ops:
  0.6 5.2 %shard_map.131 = f32[16,4,4,3,16,128]{5,4,3,2,1,0:T(8,128)S(1)} custom-call(f32[3,16,64,128]{3,2,1,0:T(8,128)} %flow_ref.1, f32[3,16,64,128]{3,2,1,0:T(8,128)} %tangent_ref.3, f32[3,16,64,128]{3,2,1,0:T(8,128)} %second_ref.3, f32[3,16,64,128]{3,2,1,0:T(8,128)} %adjoint_ref.1, bf16[4,256,256]{2,1,0:T(8,128)(2,1)} %constant.14.clone.radial_ref), custom_call_target="tpu_custom_call" | custom-call | tf_op jit(solution)/shard_map/pallas_call | solution.py:326
  5.9 0.0 copy-start
  5.9 0.0 copy-start.3
  5.9 0.0 copy-start.4
  5.9 0.0 copy-start.5
  5.9 86.4 %all_to_all.10 = f32[128,6,16,128]{3,2,1,0:T(8,128)S(1)} all-to-all(f32[128,6,16,128]{3,2,1,0:T(8,128)S(1)} %bitcast.6), channel_id=1, replica_groups=mesh['ax'=8,'az'=16] {'ax','az'}, dimensions={0} | all-to-all | bytes 12582912 | tf_op jit(solution)/shard_map/all_to_all | solution.py:376
  92.3 0.0 copy-done
  92.3 0.0 copy-start.6
  92.3 3.6 %shard_map.132 = (f32[3,256,1024]{2,1,0:T(8,128)S(1)}, f32[256,1024]{1,0:T(8,128)S(1)}) custom-call(f32[8,16,6,16,128]{4,3,2,1,0:T(8,128)S(1)} %bitcast.4, bf16[2,2,128,128]{3,2,1,0:T(8,128)(2,1)S(1)} %copy-done.5, bf16[2,256,256]{2,1,0:T(8,128)(2,1)S(1)} %copy-done.4, bf16[2,256,256]{2,1,0:T(8,128)(2,1)S(1)} %copy-done.3, bf16[2,512,512]{2,1,0:T(8,128)(2,1)S(1)} %copy-done), custom_call_target="tpu_custom_call" | custom-call | tf_op jit(solution)/shard_map/pallas_call | solution.py:326
  95.9 1.3 collective-permute-start
  97.3 5.1 %shard_map.134 = (f32[3,128,1024]{2,1,0:T(8,128)S(1)}, f32[3,128,1024]{2,1,0:T(8,128)S(1)}) custom-call(f32[8,16,6,16,128]{4,3,2,1,0:T(8,128)S(1)} %bitcast.5, f32[3,256,1024]{2,1,0:T(8,128)S(1)} %get-tuple-element.6.own_ref, f32[256,1024]{1,0:T(8,128)S(1)} %get-tuple-element.7.own_sum_ref, bf16[2,2,128,128]{3,2,1,0:T(8,128)(2,1)S(1)} %copy-done.5, ...), custom_call_target="tpu_custom_call" | custom-call | tf_op jit(solution)/shard_map/pallas_call | solution.py:326
  102.4 0.1 collective-permute-start.1
  102.5 0.1 collective-permute-done.other_ref
  102.6 2.6 %shard_map.133.tangent_ref = f32[8,16,3,8,128]{4,3,2,1,0:T(8,128)S(1)} custom-call(f32[3,256,1024]{2,1,0:T(8,128)S(1)} %get-tuple-element.6.own_ref, f32[256,1024]{1,0:T(8,128)S(1)} %get-tuple-element.7.own_sum_ref, f32[3,256,1024]{2,1,0:T(8,128)S(1)} %collective-permute-done.other_ref, bf16[2,2,2,64,128]{4,3,2,1,0:T(8,128)(2,1)S(1)} %copy-done.6, ...), custom_call_target="tpu_custom_call" | custom-call | tf_op jit(solution)/shard_map/pallas_call | solution.py:326
  105.2 0.7 collective-permute-done.1.other_ref
  105.9 1.2 shard_map.135
  107.1 0.0 copy-start.8
  107.1 0.0 copy-start.1
  107.1 0.0 copy-start.2
  107.1 0.0 copy-start.7
  107.2 45.5 %all_to_all.11 = f32[128,6,8,128]{3,2,1,0:T(8,128)S(1)} all-to-all(f32[128,6,8,128]{3,2,1,0:T(8,128)S(1)} %bitcast.7), channel_id=1, replica_groups=mesh['ax'=8,'az'=16] {'ax','az'}, dimensions={0} | all-to-all | bytes 6291456 | tf_op jit(solution)/shard_map/all_to_all | solution.py:376
  152.6 0.1 broadcast_in_dim.2.rate_ref
  152.7 0.0 copy-done.2
  152.7 2.8 %shard_map.136 = (f32[3,16,64,128]{3,2,1,0:T(8,128)}, f32[3,16,64,128]{3,2,1,0:T(8,128)}) custom-call(f32[16,4,4,3,8,128]{5,4,3,2,1,0:T(8,128)S(1)} %bitcast.8, f32[3,16,64,128]{3,2,1,0:T(8,128)S(1)} %copy-done.1, f32[3,16,64,128]{3,2,1,0:T(8,128)S(1)} %copy-done.2, f32[64,128]{1,0:T(8,128)S(1)} %broadcast_in_dim.2.rate_ref, bf16[4,256,256]{2,1,0:T(8,128)(2,1)S(1)} %copy-done.7), custom_call_target="tpu_custom_call" | custom-call | tf_op jit(solution)/shard_map/pallas_call | solution.py:326
  (7 shorter events, 0.0 us)
Async XLA Ops:
  5.9 86.5 %copy-start = (bf16[2,512,512]{2,1,0:T(8,128)(2,1)S(1)}, bf16[2,512,512]{2,1,0:T(8,128)(2,1)}, u32[]{:S(2)}) copy-start(bf16[2,512,512]{2,1,0:T(8,128)(2,1)} %constant.18.clone.odd_ref) | copy-start | bytes 3145732
  5.9 86.4 %copy-start.3 = (bf16[2,256,256]{2,1,0:T(8,128)(2,1)S(1)}, bf16[2,256,256]{2,1,0:T(8,128)(2,1)}, u32[]{:S(2)}) copy-start(bf16[2,256,256]{2,1,0:T(8,128)(2,1)} %constant.17.clone.two_ref) | copy-start | bytes 786436
  5.9 86.4 %copy-start.4 = (bf16[2,256,256]{2,1,0:T(8,128)(2,1)S(1)}, bf16[2,256,256]{2,1,0:T(8,128)(2,1)}, u32[]{:S(2)}) copy-start(bf16[2,256,256]{2,1,0:T(8,128)(2,1)} %constant.16.clone.zero_ref) | copy-start | bytes 786436
  5.9 86.4 %copy-start.5 = (bf16[2,2,128,128]{3,2,1,0:T(8,128)(2,1)S(1)}, bf16[2,2,128,128]{3,2,1,0:T(8,128)(2,1)}, u32[]{:S(2)}) copy-start(bf16[2,2,128,128]{3,2,1,0:T(8,128)(2,1)} %constant.15.clone.azimuth_ref) | copy-start | bytes 393220
  92.3 4.9 %copy-start.6 = (bf16[2,2,2,64,128]{4,3,2,1,0:T(8,128)(2,1)S(1)}, bf16[2,2,2,64,128]{4,3,2,1,0:T(8,128)(2,1)}, u32[]{:S(2)}) copy-start(bf16[2,2,2,64,128]{4,3,2,1,0:T(8,128)(2,1)} %constant.19.clone.back_ref) | copy-start | bytes 393220
  95.9 6.6 %collective-permute-start = (f32[3,256,1024]{2,1,0:T(8,128)S(1)}, f32[3,256,1024]{2,1,0:T(8,128)S(1)}, u32[]{:S(2)}, u32[]{:S(2)}) collective-permute-start(f32[3,256,1024]{2,1,0:T(8,128)S(1)} %get-tuple-element.6.own_ref), channel_id=1, source_target_pairs={{0,1},{1,0},{2,3},{3,2},{4,5},{5,4},{6,7},{7,6},{8,9},{9,8},{10,11... | collective-permute-start | bytes 9437192 | tf_op jit(solution)/shard_map/ppermute | solution.py:373
  102.4 3.5 %collective-permute-start.1 = (f32[3,128,1024]{2,1,0:T(8,128)S(1)}, f32[3,128,1024]{2,1,0:T(8,128)S(1)}, u32[]{:S(2)}, u32[]{:S(2)}) collective-permute-start(f32[3,128,1024]{2,1,0:T(8,128)S(1)} %get-tuple-element.9), channel_id=1, source_target_pairs={{0,1},{1,0},{2,3},{3,2},{4,5},{5,4},{6,7},{7,6},{8,9},{9,8},{10,11... | collective-permute-start | bytes 4718600 | tf_op jit(solution)/shard_map/ppermute | solution.py:373
  107.1 45.5 %copy-start.8 = (f32[64]{0:T(128)S(1)}, f32[64]{0:T(128)}, u32[]{:S(2)}) copy-start(f32[64]{0:T(128)} %param.16) | copy-start | bytes 772
  107.1 45.6 %copy-start.1 = (f32[3,16,64,128]{3,2,1,0:T(8,128)S(1)}, f32[3,16,64,128]{3,2,1,0:T(8,128)}, u32[]{:S(2)}) copy-start(f32[3,16,64,128]{3,2,1,0:T(8,128)} %tangent_ref.3) | copy-start | bytes 4718596
  107.1 45.6 %copy-start.2 = (f32[3,16,64,128]{3,2,1,0:T(8,128)S(1)}, f32[3,16,64,128]{3,2,1,0:T(8,128)}, u32[]{:S(2)}) copy-start(f32[3,16,64,128]{3,2,1,0:T(8,128)} %second_ref.3) | copy-start | bytes 4718596
  107.1 45.6 %copy-start.7 = (bf16[4,256,256]{2,1,0:T(8,128)(2,1)S(1)}, bf16[4,256,256]{2,1,0:T(8,128)(2,1)}, u32[]{:S(2)}) copy-start(bf16[4,256,256]{2,1,0:T(8,128)(2,1)} %constant.20.clone.table_ref) | copy-start | bytes 1572868

commit v9 on v8

--- a/solution.py
+++ b/solution.py
@@ -85,12 +85,13 @@
     adjoint_ref,
     radial_ref,
     out_ref,
+    compact_ref,
     table_ref,
     field_ref,
     sem,
     sems,
 ):
-    fetch_table = pltpu.make_async_copy(radial_ref, table_ref, sem)
+    fetch_table = pltpu.make_async_copy(radial_ref, compact_ref, sem)
 
     def fetch(i, ref, c, start):
         place = (c, pl.ds(start, 8))
@@ -106,6 +107,13 @@
             if c == start == 0:
                 fetch_table.start()
     fetch_table.wait()
+    odd = lax.broadcasted_iota(jnp.int32, (128, 128), 0) % 2
+    for p in range(4):
+        for i in range(2):
+            part = compact_ref[p, i].astype(F32)
+            for n in range(2):
+                rows, lanes = slice(128 * i, 128 * i + 128), slice(128 * n, 128 * n + 128)
+                table_ref[p, rows, lanes] = jnp.where(odd == n, part, 0.0).astype(BF16)
 
     def work(*groups):
         for place in groups:
@@ -340,10 +348,9 @@
         j = (4 * t + (p - b) % 4).ravel()
         same = n.ravel()[:, None, None] == np.arange(2)[None, :, None]
         plain = np.where(same, radial[j][:, None, :], 0.0)
-        high, low = halves(plain)
+        high, low = halves(radial[j])
         none = np.zeros_like(low)
-        rows = [np.stack(pair, axis=2).reshape(128, 256) for pair in ((high, high), (low, none))]
-        there.append(np.concatenate(rows, axis=0))
+        there.append(np.stack([np.concatenate(x, axis=1) for x in ((high, high), (low, none))]))
         back.append(stacked(plain.reshape(128, 128).T))
     return np.stack(there), np.stack(back)
 
@@ -384,6 +391,7 @@
         ),
         pltpu.with_memory_space_constraint(jnp.asarray(there), pltpu.HBM),
         scratch=(
+            pltpu.VMEM((4, 2, 128, 128), BF16),
             pltpu.VMEM((4, 256, 256), BF16),
             pltpu.VMEM((4, 3, 16, 64, 128), F32),
             pltpu.SemaphoreType.DMA,

time: 156 us -> 156 us (level)
  no operation moved by 1% of the time
where the time goes in v9:
time: 156 us; the launch traced here: 155 us
  blocking collectives  132 us (85%)
  Pallas kernels  20.4 us (13%)
    all_to_all x2, blocking collectives, whole(): return lax.all_to_all(x, ('ax', 'az'), 0, 0, tiled=True)  132 us
    pallas_call x6, Pallas kernels, call(): pl.pallas_call(kernel, out_shape=out, in_specs=specs or [WHOLE] * len(arg...  20.4 us
  transfers between devices with their start and end apart: 2, of which 2 were waited for; matrix products, arithmetic and copies ran while one was open for 0% of the time, Pallas kernels for 5%

profile of v9, /device:TPU:1, one launch (start us, length us, event | category | flops | bytes accessed | tf_op | source)
XLA Modules:
  0.0 155.4 jit_solution(1223051523050468298)
XLA Ops:
  0.6 5.1 %shard_map.131 = f32[16,4,4,3,16,128]{5,4,3,2,1,0:T(8,128)S(1)} custom-call(f32[3,16,64,128]{3,2,1,0:T(8,128)} %flow_ref.1, f32[3,16,64,128]{3,2,1,0:T(8,128)} %tangent_ref.3, f32[3,16,64,128]{3,2,1,0:T(8,128)} %second_ref.3, f32[3,16,64,128]{3,2,1,0:T(8,128)} %adjoint_ref.1, bf16[4,2,128,128]{3,2,1,0:T(8,128)(2,1)} %constant.14.clone.radial_ref), custom_call_target="tpu_custom_call" | custom-call | tf_op jit(solution)/shard_map/pallas_call | solution.py:334
  5.8 0.0 copy-start
  5.8 0.0 copy-start.3
  5.8 0.0 copy-start.4
  5.8 0.0 copy-start.5
  5.8 86.4 %all_to_all.10 = f32[128,6,16,128]{3,2,1,0:T(8,128)S(1)} all-to-all(f32[128,6,16,128]{3,2,1,0:T(8,128)S(1)} %bitcast.6), channel_id=1, replica_groups=mesh['ax'=8,'az'=16] {'ax','az'}, dimensions={0} | all-to-all | bytes 12582912 | tf_op jit(solution)/shard_map/all_to_all | solution.py:383
  92.2 0.0 copy-done.5
  92.3 0.0 copy-start.6
  92.3 3.6 %shard_map.132 = (f32[3,256,1024]{2,1,0:T(8,128)S(1)}, f32[256,1024]{1,0:T(8,128)S(1)}) custom-call(f32[8,16,6,16,128]{4,3,2,1,0:T(8,128)S(1)} %bitcast.4, bf16[2,2,128,128]{3,2,1,0:T(8,128)(2,1)S(1)} %copy-done.5, bf16[2,256,256]{2,1,0:T(8,128)(2,1)S(1)} %copy-done.4, bf16[2,256,256]{2,1,0:T(8,128)(2,1)S(1)} %copy-done.3, bf16[2,512,512]{2,1,0:T(8,128)(2,1)S(1)} %copy-done), custom_call_target="tpu_custom_call" | custom-call | tf_op jit(solution)/shard_map/pallas_call | solution.py:334
  95.9 1.4 collective-permute-start
  97.2 5.1 %shard_map.134 = (f32[3,128,1024]{2,1,0:T(8,128)S(1)}, f32[3,128,1024]{2,1,0:T(8,128)S(1)}) custom-call(f32[8,16,6,16,128]{4,3,2,1,0:T(8,128)S(1)} %bitcast.5, f32[3,256,1024]{2,1,0:T(8,128)S(1)} %get-tuple-element.6.own_ref, f32[256,1024]{1,0:T(8,128)S(1)} %get-tuple-element.7.own_sum_ref, bf16[2,2,128,128]{3,2,1,0:T(8,128)(2,1)S(1)} %copy-done.5, ...), custom_call_target="tpu_custom_call" | custom-call | tf_op jit(solution)/shard_map/pallas_call | solution.py:334
  102.3 0.1 collective-permute-start.1
  102.4 0.1 collective-permute-done.other_ref
  102.5 2.6 %shard_map.133.tangent_ref = f32[8,16,3,8,128]{4,3,2,1,0:T(8,128)S(1)} custom-call(f32[3,256,1024]{2,1,0:T(8,128)S(1)} %get-tuple-element.6.own_ref, f32[256,1024]{1,0:T(8,128)S(1)} %get-tuple-element.7.own_sum_ref, f32[3,256,1024]{2,1,0:T(8,128)S(1)} %collective-permute-done.other_ref, bf16[2,2,2,64,128]{4,3,2,1,0:T(8,128)(2,1)S(1)} %copy-done.6, ...), custom_call_target="tpu_custom_call" | custom-call | tf_op jit(solution)/shard_map/pallas_call | solution.py:334
  105.1 0.7 collective-permute-done.1.other_ref
  105.8 1.2 shard_map.135
  107.0 0.0 copy-start.8
  107.1 0.0 copy-start.1
  107.1 0.0 copy-start.2
  107.1 0.0 copy-start.7
  107.1 45.5 %all_to_all.11 = f32[128,6,8,128]{3,2,1,0:T(8,128)S(1)} all-to-all(f32[128,6,8,128]{3,2,1,0:T(8,128)S(1)} %bitcast.7), channel_id=1, replica_groups=mesh['ax'=8,'az'=16] {'ax','az'}, dimensions={0} | all-to-all | bytes 6291456 | tf_op jit(solution)/shard_map/all_to_all | solution.py:383
  152.6 0.1 broadcast_in_dim.2.rate_ref
  152.6 0.0 copy-done.1
  152.7 2.8 %shard_map.136 = (f32[3,16,64,128]{3,2,1,0:T(8,128)}, f32[3,16,64,128]{3,2,1,0:T(8,128)}) custom-call(f32[16,4,4,3,8,128]{5,4,3,2,1,0:T(8,128)S(1)} %bitcast.8, f32[3,16,64,128]{3,2,1,0:T(8,128)S(1)} %copy-done.1, f32[3,16,64,128]{3,2,1,0:T(8,128)S(1)} %copy-done.2, f32[64,128]{1,0:T(8,128)S(1)} %broadcast_in_dim.2.rate_ref, bf16[4,256,256]{2,1,0:T(8,128)(2,1)S(1)} %copy-done.7), custom_call_target="tpu_custom_call" | custom-call | tf_op jit(solution)/shard_map/pallas_call | solution.py:334
  (7 shorter events, 0.0 us)
Async XLA Ops:
  5.8 86.5 %copy-start = (bf16[2,512,512]{2,1,0:T(8,128)(2,1)S(1)}, bf16[2,512,512]{2,1,0:T(8,128)(2,1)}, u32[]{:S(2)}) copy-start(bf16[2,512,512]{2,1,0:T(8,128)(2,1)} %constant.18.clone.odd_ref) | copy-start | bytes 3145732
  5.8 86.5 %copy-start.3 = (bf16[2,256,256]{2,1,0:T(8,128)(2,1)S(1)}, bf16[2,256,256]{2,1,0:T(8,128)(2,1)}, u32[]{:S(2)}) copy-start(bf16[2,256,256]{2,1,0:T(8,128)(2,1)} %constant.17.clone.two_ref) | copy-start | bytes 786436
  5.8 86.4 %copy-start.4 = (bf16[2,256,256]{2,1,0:T(8,128)(2,1)S(1)}, bf16[2,256,256]{2,1,0:T(8,128)(2,1)}, u32[]{:S(2)}) copy-start(bf16[2,256,256]{2,1,0:T(8,128)(2,1)} %constant.16.clone.zero_ref) | copy-start | bytes 786436
  5.8 86.4 %copy-start.5 = (bf16[2,2,128,128]{3,2,1,0:T(8,128)(2,1)S(1)}, bf16[2,2,128,128]{3,2,1,0:T(8,128)(2,1)}, u32[]{:S(2)}) copy-start(bf16[2,2,128,128]{3,2,1,0:T(8,128)(2,1)} %constant.15.clone.azimuth_ref) | copy-start | bytes 393220
  92.3 5.0 %copy-start.6 = (bf16[2,2,2,64,128]{4,3,2,1,0:T(8,128)(2,1)S(1)}, bf16[2,2,2,64,128]{4,3,2,1,0:T(8,128)(2,1)}, u32[]{:S(2)}) copy-start(bf16[2,2,2,64,128]{4,3,2,1,0:T(8,128)(2,1)} %constant.19.clone.back_ref) | copy-start | bytes 393220
  95.9 6.6 %collective-permute-start = (f32[3,256,1024]{2,1,0:T(8,128)S(1)}, f32[3,256,1024]{2,1,0:T(8,128)S(1)}, u32[]{:S(2)}, u32[]{:S(2)}) collective-permute-start(f32[3,256,1024]{2,1,0:T(8,128)S(1)} %get-tuple-element.6.own_ref), channel_id=1, source_target_pairs={{0,1},{1,0},{2,3},{3,2},{4,5},{5,4},{6,7},{7,6},{8,9},{9,8},{10,11... | collective-permute-start | bytes 9437192 | tf_op jit(solution)/shard_map/ppermute | solution.py:380
  102.3 3.5 %collective-permute-start.1 = (f32[3,128,1024]{2,1,0:T(8,128)S(1)}, f32[3,128,1024]{2,1,0:T(8,128)S(1)}, u32[]{:S(2)}, u32[]{:S(2)}) collective-permute-start(f32[3,128,1024]{2,1,0:T(8,128)S(1)} %get-tuple-element.9), channel_id=1, source_target_pairs={{0,1},{1,0},{2,3},{3,2},{4,5},{5,4},{6,7},{7,6},{8,9},{9,8},{10,11... | collective-permute-start | bytes 4718600 | tf_op jit(solution)/shard_map/ppermute | solution.py:380
  107.0 45.5 %copy-start.8 = (f32[64]{0:T(128)S(1)}, f32[64]{0:T(128)}, u32[]{:S(2)}) copy-start(f32[64]{0:T(128)} %param.16) | copy-start | bytes 772
  107.1 45.6 %copy-start.1 = (f32[3,16,64,128]{3,2,1,0:T(8,128)S(1)}, f32[3,16,64,128]{3,2,1,0:T(8,128)}, u32[]{:S(2)}) copy-start(f32[3,16,64,128]{3,2,1,0:T(8,128)} %tangent_ref.3) | copy-start | bytes 4718596
  107.1 45.6 %copy-start.2 = (f32[3,16,64,128]{3,2,1,0:T(8,128)S(1)}, f32[3,16,64,128]{3,2,1,0:T(8,128)}, u32[]{:S(2)}) copy-start(f32[3,16,64,128]{3,2,1,0:T(8,128)} %second_ref.3) | copy-start | bytes 4718596
  107.1 45.6 %copy-start.7 = (bf16[4,256,256]{2,1,0:T(8,128)(2,1)S(1)}, bf16[4,256,256]{2,1,0:T(8,128)(2,1)}, u32[]{:S(2)}) copy-start(bf16[4,256,256]{2,1,0:T(8,128)(2,1)} %constant.20.clone.table_ref) | copy-start | bytes 1572868
